TPU v7x, 32 devices: a whole 2x2x4 slice. The times are simulated.
32 devices in a mesh: fsdp: 8 (over y, x, core), rep: 4 (over z).
Axes of the slice: x: 2, y: 2, z: 4, core: 2. Of those that a mesh axis runs over, the one named last changes fastest.
Arguments:
- frames: bfloat16 [32, 1024, 768], P(('fsdp', 'rep')), may hold values from -6 to 6
- tokens: bfloat16 [32, 448, 768], P(('fsdp', 'rep')), may hold values from -6 to 6
- memory: bfloat16 [32, 1024, 768], P(('fsdp', 'rep')), may hold values from -6 to 6
- segment_ids: int32 [32, 448], P(('fsdp', 'rep')), may hold values from 0 to 3, never falling along the last dimension, each value on 1 to 224 neighbouring positions
- enc_attn: float32 [4, 768, 768], P(None, ('fsdp', 'rep')), may hold values from -1 to 1
- enc_up: float32 [768, 3072], P(('fsdp', 'rep')), may hold values from -0.21875 to 0.21875
- enc_down: float32 [3072, 768], P(('fsdp', 'rep')), may hold values from -0.109375 to 0.109375
- enc_vec: float32 [8, 768], P(None, ('fsdp', 'rep')), may hold values from -1.2 to 1.4
- enc_up_bias: float32 [3072], P(('fsdp', 'rep')), may hold values from -1.2 to 1.2
- dec_attn: float32 [8, 768, 768], P(None, ('fsdp', 'rep')), may hold values from -1 to 1
- dec_up: float32 [768, 3072], P(('fsdp', 'rep')), may hold values from -0.21875 to 0.21875
- dec_down: float32 [3072, 768], P(('fsdp', 'rep')), may hold values from -0.109375 to 0.109375
- dec_vec: float32 [12, 768], P(None, ('fsdp', 'rep')), may hold values from -1.2 to 1.4
- dec_up_bias: float32 [3072], P(('fsdp', 'rep')), may hold values from -1.2 to 1.2
- dec_down_bias: float32 [768], P(('fsdp', 'rep')), may hold values from -1.2 to 1.2
- enc_out_grad: float32 [32, 1024, 768], P(('fsdp', 'rep')), may hold values from -6 to 6
- dec_out_grad: float32 [32, 448, 768], P(('fsdp', 'rep')), may hold values from -6 to 6
Outputs:
- enc_out: float32 [32, 1024, 768], P(('fsdp', 'rep'))
- dec_out: float32 [32, 448, 768], P(('fsdp', 'rep'))
- frames_grad: float32 [32, 1024, 768], P(('fsdp', 'rep'))
- tokens_grad: float32 [32, 448, 768], P(('fsdp', 'rep'))
- memory_grad: float32 [32, 1024, 768], P(('fsdp', 'rep'))
- enc_attn_grad: float32 [4, 768, 768], P(None, ('fsdp', 'rep'))
- enc_up_grad: float32 [768, 3072], P(('fsdp', 'rep'))
- enc_down_grad: float32 [3072, 768], P(('fsdp', 'rep'))
- enc_vec_grad: float32 [8, 768], P(None, ('fsdp', 'rep'))
- enc_up_bias_grad: float32 [3072], P(('fsdp', 'rep'))
- dec_attn_grad: float32 [8, 768, 768], P(None, ('fsdp', 'rep'))
- dec_up_grad: float32 [768, 3072], P(('fsdp', 'rep'))
- dec_down_grad: float32 [3072, 768], P(('fsdp', 'rep'))
- dec_vec_grad: float32 [12, 768], P(None, ('fsdp', 'rep'))
- dec_up_bias_grad: float32 [3072], P(('fsdp', 'rep'))
- dec_down_bias_grad: float32 [768], P(('fsdp', 'rep'))
Inputs may be any that keep to these rules, and one draw needn't show every extreme that they name: `segment_ids`: along each row the ids never fall; each of the 4 transcripts holds 1 to 224 tokens, and one holds exactly that many.
All inputs are finite; a program needn't handle non-finite values.
Results may differ from a plain program's by a relative error of at most 0.025.
The roundings to bfloat16 on the way count: a program that leaves them out, or rounds other values in their place, can miss the bound.
Values may be sent and summed in bfloat16 or wider, within the bound.
A program may use at most 320 MiB of HBM per device.

v0:
```python
import jax
import jax.numpy as jnp
from jax import lax
from jax.sharding import PartitionSpec as P

HEADS = 12


epsilon = 1e-05
masked_score = -1e30


def matmul(left, right):
    return jnp.dot(left, right, preferred_element_type=jnp.float32)


def left_product(left, right):
    return lax.dot_general(
        left, right, (((0,), (0,)), ((), ())), preferred_element_type=jnp.float32
    )


def right_product(left, right):
    return lax.dot_general(
        left, right, (((1,), (1,)), ((), ())), preferred_element_type=jnp.float32
    )


def layer_norm(inputs, gain, shift):
    center = inputs - jnp.mean(inputs, -1, keepdims=True)
    spread = jnp.mean(center * center, -1, keepdims=True)
    return center * lax.rsqrt(spread + epsilon) * gain + shift


def norm_back(inputs, gain, shift, upstream):
    pull = jax.vjp(layer_norm, inputs, gain, shift)[1]
    return pull(upstream)


def gelu_exact(inputs):
    return jax.nn.gelu(inputs, approximate=False)


def open_mask(scores, first_row):
    return scores


def segment_mask(segment_row):
    key_index = jnp.arange(segment_row.shape[0], dtype=jnp.int32)

    def apply_mask(scores, first_row):
        block_rows = scores.shape[1]
        query_index = first_row + jnp.arange(block_rows, dtype=jnp.int32)
        allowed = (segment_row[:, None] == segment_row[None, :]) & (
            key_index[None, :] <= query_index[:, None]
        )
        return jnp.where(allowed[None], scores, masked_score)

    return apply_mask


def attend_forward(queries, keys_in, values_in, masking):
    row_count, model_width = queries.shape
    head_dim = model_width // HEADS
    block_rows = min(512, row_count)
    key_heads = keys_in.reshape(-1, HEADS, head_dim)
    value_heads = values_in.reshape(-1, HEADS, head_dim)

    def one_block(block_index):
        first_row = block_index * block_rows
        query_block = lax.dynamic_slice_in_dim(queries, first_row, block_rows, 0).reshape(
            block_rows, HEADS, head_dim
        )
        scores = masking(
            jnp.einsum("qhd,khd->hqk", query_block, key_heads, preferred_element_type=jnp.float32),
            first_row,
        )
        row_max = jnp.max(scores, -1, keepdims=True)
        exp_scores = jnp.exp(scores - row_max)
        row_sum = jnp.sum(exp_scores, -1, keepdims=True)
        attn_probs = (exp_scores / row_sum).astype(jnp.bfloat16)
        context = jnp.einsum(
            "hqk,khd->qhd", attn_probs, value_heads, preferred_element_type=jnp.float32
        )
        return (
            context.reshape(block_rows, model_width).astype(jnp.bfloat16),
            (row_max + jnp.log(row_sum))[..., 0],
        )

    context, log_sums = lax.map(one_block, jnp.arange(row_count // block_rows, dtype=jnp.int32))
    return (context.reshape(row_count, model_width), log_sums)


def attend_backward(queries, keys_in, values_in, log_sums, grad_context, masking):
    row_count, model_width = queries.shape
    head_dim = model_width // HEADS
    block_rows = min(512, row_count)
    key_heads = keys_in.reshape(-1, HEADS, head_dim)
    value_heads = values_in.reshape(-1, HEADS, head_dim)
    zero_heads = jnp.zeros(key_heads.shape, jnp.float32)

    def one_block(carry, block_items):
        key_grad, value_grad = carry
        block_index, block_sums = block_items
        first_row = block_index * block_rows
        query_block = lax.dynamic_slice_in_dim(queries, first_row, block_rows, 0).reshape(
            block_rows, HEADS, head_dim
        )
        grad_block = lax.dynamic_slice_in_dim(grad_context, first_row, block_rows, 0).reshape(
            block_rows, HEADS, head_dim
        )
        scores = masking(
            jnp.einsum("qhd,khd->hqk", query_block, key_heads, preferred_element_type=jnp.float32),
            first_row,
        )
        attn_probs = jnp.exp(scores - block_sums[..., None])
        grad_probs = jnp.einsum(
            "qhd,khd->hqk", grad_block, value_heads, preferred_element_type=jnp.float32
        )
        grad_scores = attn_probs * (
            grad_probs - jnp.sum(attn_probs * grad_probs, -1, keepdims=True)
        )
        grad_scores = grad_scores.astype(jnp.bfloat16)
        rounded_probs = attn_probs.astype(jnp.bfloat16)
        query_grad = jnp.einsum(
            "hqk,khd->qhd", grad_scores, key_heads, preferred_element_type=jnp.float32
        )
        key_grad = key_grad + jnp.einsum(
            "hqk,qhd->khd", grad_scores, query_block, preferred_element_type=jnp.float32
        )
        value_grad = value_grad + jnp.einsum(
            "hqk,qhd->khd", rounded_probs, grad_block, preferred_element_type=jnp.float32
        )
        return ((key_grad, value_grad), query_grad.reshape(block_rows, model_width))

    block_ids = jnp.arange(row_count // block_rows, dtype=jnp.int32)
    (key_grad, value_grad), query_grad = lax.scan(
        one_block, (zero_heads, zero_heads), (block_ids, log_sums)
    )
    return (
        query_grad.reshape(row_count, model_width),
        key_grad.reshape(-1, model_width),
        value_grad.reshape(-1, model_width),
    )


def attention_forward(normed, source, stack, first_slot, vecs, first_vec, masking):
    scale = (normed.shape[1] // HEADS) ** (-0.5)
    queries = ((matmul(normed, stack[first_slot]) + vecs[first_vec]) * scale).astype(jnp.bfloat16)
    keys_out = matmul(source, stack[first_slot + 1]).astype(jnp.bfloat16)
    values_out = (matmul(source, stack[first_slot + 2]) + vecs[first_vec + 1]).astype(jnp.bfloat16)
    context, log_sums = attend_forward(queries, keys_out, values_out, masking)
    branch = matmul(context, stack[first_slot + 3]) + vecs[first_vec + 2]
    return (branch, (queries, keys_out, values_out, context, log_sums))


def attention_backward(normed, source, stack, first_slot, kept, upstream, masking):
    queries, keys_out, values_out, context, log_sums = kept
    scale = (normed.shape[1] // HEADS) ** (-0.5)
    grad_out = upstream.astype(jnp.bfloat16)
    out_grad = left_product(context, grad_out)
    out_bias_grad = jnp.sum(grad_out, 0, dtype=jnp.float32)
    grad_context = right_product(grad_out, stack[first_slot + 3]).astype(jnp.bfloat16)
    query_grad, key_grad, value_grad = attend_backward(
        queries, keys_out, values_out, log_sums, grad_context, masking
    )
    query_grad = query_grad.astype(jnp.bfloat16) * scale
    key_grad = key_grad.astype(jnp.bfloat16)
    value_grad = value_grad.astype(jnp.bfloat16)
    mat_grads = [
        left_product(normed, query_grad),
        left_product(source, key_grad),
        left_product(source, value_grad),
        out_grad,
    ]
    bias_grads = [
        jnp.sum(query_grad, 0, dtype=jnp.float32),
        jnp.sum(value_grad, 0, dtype=jnp.float32),
        out_bias_grad,
    ]
    grad_normed = right_product(query_grad, stack[first_slot])
    grad_source = right_product(key_grad, stack[first_slot + 1]) + right_product(
        value_grad, stack[first_slot + 2]
    )
    return (grad_normed, grad_source, mat_grads, bias_grads)


def mlp_forward(normed, up_proj, up_bias, down_proj, down_bias):
    pre_act = matmul(normed, up_proj) + up_bias
    hidden = gelu_exact(pre_act).astype(jnp.bfloat16)
    return (matmul(hidden, down_proj) + down_bias, pre_act)


def mlp_backward(normed, pre_act, up_proj, down_proj, upstream):
    grad_out = upstream.astype(jnp.bfloat16)
    hidden = gelu_exact(pre_act).astype(jnp.bfloat16)
    down_grad = left_product(hidden, grad_out)
    down_bias_grad = jnp.sum(grad_out, 0, dtype=jnp.float32)
    grad_hidden = right_product(grad_out, down_proj)
    grad_pre = jax.vjp(gelu_exact, pre_act)[1](grad_hidden)[0].astype(jnp.bfloat16)
    up_grad = left_product(normed, grad_pre)
    up_bias_grad = jnp.sum(grad_pre, 0, dtype=jnp.float32)
    grad_normed = right_product(grad_pre, up_proj)
    return (grad_normed, up_grad, up_bias_grad, down_grad, down_bias_grad)


def encoder_forward(inputs, weights):
    stack, up_proj, down_proj, vec_table, up_bias = weights
    vecs = vec_table.astype(jnp.float32)
    normed = layer_norm(inputs, vecs[0], vecs[1]).astype(jnp.bfloat16)
    branch, attn_kept = attention_forward(normed, normed, stack, 0, vecs, 2, open_mask)
    middle = inputs + branch
    mlp_normed = layer_norm(middle, vecs[5], vecs[6]).astype(jnp.bfloat16)
    mlp_out, pre_act = mlp_forward(
        mlp_normed, up_proj, up_bias.astype(jnp.float32), down_proj, vecs[7]
    )
    return (middle + mlp_out, (normed, middle, mlp_normed, pre_act, attn_kept))


def encoder_backward(inputs, kept, weights, upstream):
    stack, up_proj, down_proj, vec_table, up_bias = weights
    vecs = vec_table.astype(jnp.float32)
    normed, middle, mlp_normed, pre_act, attn_kept = kept
    grad_mlp_normed, up_grad, up_bias_grad, down_grad, down_bias_grad = mlp_backward(
        mlp_normed, pre_act, up_proj, down_proj, upstream
    )
    grad_middle, gain_two, shift_two = norm_back(middle, vecs[5], vecs[6], grad_mlp_normed)
    grad_middle = grad_middle + upstream
    grad_normed, grad_source, mat_grads, bias_grads = attention_backward(
        normed, normed, stack, 0, attn_kept, grad_middle, open_mask
    )
    grad_inputs, gain_one, shift_one = norm_back(
        inputs, vecs[0], vecs[1], grad_normed + grad_source
    )
    grad_inputs = grad_inputs + grad_middle
    vec_grad = jnp.stack(
        [
            gain_one,
            shift_one,
            bias_grads[0],
            bias_grads[1],
            bias_grads[2],
            gain_two,
            shift_two,
            down_bias_grad,
        ]
    )
    return (grad_inputs, (jnp.stack(mat_grads), up_grad, down_grad, vec_grad, up_bias_grad))


def decoder_forward(inputs, memory_row, masking, weights):
    stack, up_proj, down_proj, vec_table, up_bias, down_bias = weights
    vecs = vec_table.astype(jnp.float32)
    normed = layer_norm(inputs, vecs[0], vecs[1]).astype(jnp.bfloat16)
    self_branch, self_kept = attention_forward(normed, normed, stack, 0, vecs, 2, masking)
    first_mid = inputs + self_branch
    cross_normed = layer_norm(first_mid, vecs[5], vecs[6]).astype(jnp.bfloat16)
    cross_branch, cross_kept = attention_forward(
        cross_normed, memory_row, stack, 4, vecs, 7, open_mask
    )
    second_mid = first_mid + cross_branch
    mlp_normed = layer_norm(second_mid, vecs[10], vecs[11]).astype(jnp.bfloat16)
    mlp_out, pre_act = mlp_forward(
        mlp_normed, up_proj, up_bias.astype(jnp.float32), down_proj, down_bias.astype(jnp.float32)
    )
    kept = (normed, self_kept, first_mid, cross_normed, cross_kept, second_mid, mlp_normed, pre_act)
    return (second_mid + mlp_out, kept)


def decoder_backward(inputs, memory_row, masking, kept, weights, upstream):
    stack, up_proj, down_proj, vec_table, up_bias, down_bias = weights
    vecs = vec_table.astype(jnp.float32)
    normed, self_kept, first_mid, cross_normed, cross_kept, second_mid, mlp_normed, pre_act = kept
    grad_mlp_normed, up_grad, up_bias_grad, down_grad, down_bias_grad = mlp_backward(
        mlp_normed, pre_act, up_proj, down_proj, upstream
    )
    grad_second, gain_three, shift_three = norm_back(
        second_mid, vecs[10], vecs[11], grad_mlp_normed
    )
    grad_second = grad_second + upstream
    grad_cross, grad_memory, cross_mats, cross_biases = attention_backward(
        cross_normed, memory_row, stack, 4, cross_kept, grad_second, open_mask
    )
    grad_first, gain_two, shift_two = norm_back(first_mid, vecs[5], vecs[6], grad_cross)
    grad_first = grad_first + grad_second
    grad_normed, grad_source, self_mats, self_biases = attention_backward(
        normed, normed, stack, 0, self_kept, grad_first, masking
    )
    grad_inputs, gain_one, shift_one = norm_back(
        inputs, vecs[0], vecs[1], grad_normed + grad_source
    )
    grad_inputs = grad_inputs + grad_first
    vec_grad = jnp.stack(
        [
            gain_one,
            shift_one,
            self_biases[0],
            self_biases[1],
            self_biases[2],
            gain_two,
            shift_two,
            cross_biases[0],
            cross_biases[1],
            cross_biases[2],
            gain_three,
            shift_three,
        ]
    )
    return (
        grad_inputs,
        grad_memory,
        (
            jnp.stack(self_mats + cross_mats),
            up_grad,
            down_grad,
            vec_grad,
            up_bias_grad,
            down_bias_grad,
        ),
    )


def body(
    frames,
    tokens,
    memory,
    segment_ids,
    enc_attn,
    enc_up,
    enc_down,
    enc_vec,
    enc_up_bias,
    dec_attn,
    dec_up,
    dec_down,
    dec_vec,
    dec_up_bias,
    dec_down_bias,
    enc_out_grad,
    dec_out_grad,
):
    enc_attn_b = enc_attn.astype(jnp.bfloat16)
    enc_up_b = enc_up.astype(jnp.bfloat16)
    enc_down_b = enc_down.astype(jnp.bfloat16)
    enc_vec_b = enc_vec.astype(jnp.bfloat16)
    enc_bias_b = enc_up_bias.astype(jnp.bfloat16)
    dec_attn_b = dec_attn.astype(jnp.bfloat16)
    dec_up_b = dec_up.astype(jnp.bfloat16)
    dec_down_b = dec_down.astype(jnp.bfloat16)
    dec_vec_b = dec_vec.astype(jnp.bfloat16)
    dec_bias_b = dec_up_bias.astype(jnp.bfloat16)
    dec_down_bias_b = dec_down_bias.astype(jnp.bfloat16)
    enc_weights = (
        lax.all_gather(enc_attn_b, ("fsdp", "rep"), axis=1, tiled=True),
        lax.all_gather(enc_up_b, ("fsdp", "rep"), axis=0, tiled=True),
        lax.all_gather(enc_down_b, ("fsdp", "rep"), axis=0, tiled=True),
        lax.all_gather(enc_vec_b, ("fsdp", "rep"), axis=1, tiled=True),
        lax.all_gather(enc_bias_b, ("fsdp", "rep"), axis=0, tiled=True),
    )
    enc_inputs = frames[0].astype(jnp.float32)
    enc_result, enc_kept = encoder_forward(enc_inputs, enc_weights)
    dec_weights = (
        lax.all_gather(dec_attn_b, ("fsdp", "rep"), axis=1, tiled=True),
        lax.all_gather(dec_up_b, ("fsdp", "rep"), axis=0, tiled=True),
        lax.all_gather(dec_down_b, ("fsdp", "rep"), axis=0, tiled=True),
        lax.all_gather(dec_vec_b, ("fsdp", "rep"), axis=1, tiled=True),
        lax.all_gather(dec_bias_b, ("fsdp", "rep"), axis=0, tiled=True),
        lax.all_gather(dec_down_bias_b, ("fsdp", "rep"), axis=0, tiled=True),
    )
    dec_inputs = tokens[0].astype(jnp.float32)
    memory_row = memory[0]
    masking = segment_mask(segment_ids[0])
    dec_result, dec_kept = decoder_forward(dec_inputs, memory_row, masking, dec_weights)
    dec_back = (
        lax.all_gather(dec_attn_b, ("fsdp", "rep"), axis=1, tiled=True),
        lax.all_gather(dec_up_b, ("fsdp", "rep"), axis=0, tiled=True),
        lax.all_gather(dec_down_b, ("fsdp", "rep"), axis=0, tiled=True),
        lax.all_gather(dec_vec_b, ("fsdp", "rep"), axis=1, tiled=True),
        lax.all_gather(dec_bias_b, ("fsdp", "rep"), axis=0, tiled=True),
        lax.all_gather(dec_down_bias_b, ("fsdp", "rep"), axis=0, tiled=True),
    )
    enc_back = (
        lax.all_gather(enc_attn_b, ("fsdp", "rep"), axis=1, tiled=True),
        lax.all_gather(enc_up_b, ("fsdp", "rep"), axis=0, tiled=True),
        lax.all_gather(enc_down_b, ("fsdp", "rep"), axis=0, tiled=True),
        lax.all_gather(enc_vec_b, ("fsdp", "rep"), axis=1, tiled=True),
        lax.all_gather(enc_bias_b, ("fsdp", "rep"), axis=0, tiled=True),
    )
    tokens_grad, memory_grad, dec_parts = decoder_backward(
        dec_inputs, memory_row, masking, dec_kept, dec_back, dec_out_grad[0]
    )
    dec_mlp = (
        lax.psum_scatter(dec_parts[1], ("fsdp", "rep"), scatter_dimension=0, tiled=True),
        lax.psum_scatter(dec_parts[2], ("fsdp", "rep"), scatter_dimension=0, tiled=True),
        lax.psum_scatter(dec_parts[4], ("fsdp", "rep"), scatter_dimension=0, tiled=True),
        lax.psum_scatter(dec_parts[5], ("fsdp", "rep"), scatter_dimension=0, tiled=True),
    )
    dec_rest = (
        lax.psum_scatter(dec_parts[0], ("fsdp", "rep"), scatter_dimension=1, tiled=True),
        lax.psum_scatter(dec_parts[3], ("fsdp", "rep"), scatter_dimension=1, tiled=True),
    )
    frames_grad, enc_parts = encoder_backward(enc_inputs, enc_kept, enc_back, enc_out_grad[0])
    enc_mlp = (
        lax.psum_scatter(enc_parts[1], ("fsdp", "rep"), scatter_dimension=0, tiled=True),
        lax.psum_scatter(enc_parts[2], ("fsdp", "rep"), scatter_dimension=0, tiled=True),
        lax.psum_scatter(enc_parts[4], ("fsdp", "rep"), scatter_dimension=0, tiled=True),
    )
    enc_rest = (
        lax.psum_scatter(enc_parts[0], ("fsdp", "rep"), scatter_dimension=1, tiled=True),
        lax.psum_scatter(enc_parts[3], ("fsdp", "rep"), scatter_dimension=1, tiled=True),
    )
    return (
        enc_result[None],
        dec_result[None],
        frames_grad[None],
        tokens_grad[None],
        memory_grad[None],
        enc_rest[0],
        enc_mlp[0],
        enc_mlp[1],
        enc_rest[1],
        enc_mlp[2],
        dec_rest[0],
        dec_mlp[0],
        dec_mlp[1],
        dec_rest[1],
        dec_mlp[2],
        dec_mlp[3],
    )


def solution(mesh):
    placed = (
        P(("fsdp", "rep"), None, None),
        P(("fsdp", "rep"), None, None),
        P(("fsdp", "rep"), None, None),
        P(("fsdp", "rep"), None),
        P(None, ("fsdp", "rep"), None),
        P(("fsdp", "rep"), None),
        P(("fsdp", "rep"), None),
        P(None, ("fsdp", "rep")),
        P(("fsdp", "rep")),
        P(None, ("fsdp", "rep"), None),
        P(("fsdp", "rep"), None),
        P(("fsdp", "rep"), None),
        P(None, ("fsdp", "rep")),
        P(("fsdp", "rep")),
        P(("fsdp", "rep")),
        P(("fsdp", "rep"), None, None),
        P(("fsdp", "rep"), None, None),
    )
    return jax.shard_map(
        body,
        mesh=mesh,
        in_specs=placed,
        out_specs=(
            P(("fsdp", "rep"), None, None),
            P(("fsdp", "rep"), None, None),
            P(("fsdp", "rep"), None, None),
            P(("fsdp", "rep"), None, None),
            P(("fsdp", "rep"), None, None),
            P(None, ("fsdp", "rep"), None),
            P(("fsdp", "rep"), None),
            P(("fsdp", "rep"), None),
            P(None, ("fsdp", "rep")),
            P(("fsdp", "rep")),
            P(None, ("fsdp", "rep"), None),
            P(("fsdp", "rep"), None),
            P(("fsdp", "rep"), None),
            P(None, ("fsdp", "rep")),
            P(("fsdp", "rep")),
            P(("fsdp", "rep")),
        ),
        check_vma=False,
    )
```

profile of v0, /device:TPU:0, one launch (start us, length us, event | category | flops | bytes accessed | tf_op | source)
XLA Modules:
  0.0 1834.4 jit_solution(3719788415540655470)
XLA Ops:
  18.0 42.3 %all-reduce.9 = (bf16[3072]{0:T(1024)(128)(2,1)S(1)}, bf16[3072]{0:T(1024)(128)(2,1)S(1)}, bf16[768]{0:T(1024)(128)(2,1)}) all-reduce(bf16[3072]{0:T(1024)(128)(2,1)S(1)} %dynamic-update-slice, bf16[3072]{0:T(1024)(128)(2,1)S(1)} %dynamic-update-slice.1, ...), channel_id=1, replica_groups=mesh['fsdp'=8,'rep'=4] {'fsdp','rep'}, use_global_device_ids=true, to_apply=%add | all-reduce | flops 6912 | bytes 27648
  61.6 67.4 %all-gather = bf16[32,24,8]{1,2,0:T(8,128)(2,1)S(1)} all-gather(bf16[1,24,8]{1,2,0:T(8,128)(2,1)S(1)} %convert_bitcast_fusion.3), channel_id=1, replica_groups=mesh['fsdp'=8,'rep'=4] {'fsdp','rep'}, dimensions={0}, use_global_device_ids=true | all-gather | bytes 12672 | tf_op jit(solution)/shard_map/all_gather | solution.py:357
  130.0 65.0 %all-gather.1 = bf16[32,24,12]{1,2,0:T(8,128)(2,1)S(1)} all-gather(bf16[1,24,12]{1,2,0:T(8,128)(2,1)S(1)} %convert_bitcast_fusion.2), channel_id=1, replica_groups=mesh['fsdp'=8,'rep'=4] {'fsdp','rep'}, dimensions={0}, use_global_device_ids=true | all-gather | bytes 19008 | tf_op jit(solution)/shard_map/all_gather | solution.py:366
  217.5 80.7 %while.5 = (s32[]{:T(128)}, bf16[2,512,768]{2,1,0:T(8,128)(2,1)}, f32[2,12,512]{2,1,0:T(8,128)S(1)}, s32[2]{0:T(128)S(1)}, bf16[1024,768]{0,1:T(8,128)(2,1)}, /*...) while((s32[]{:T(128)}, bf16[2,512,768]{2,1,0:T(8,128)(2,1)}, ...), condition=%wide.region_5.6_spmd, body=%wide.region_2.5_spmd.sunk | while | flops 1648748544 | bytes 91447504 | solution.py:90
  220.0 10.1 fusion.259
  230.1 11.0 fusion.260
  241.2 11.3 fusion.261
  259.2 11.2 fusion.259
  270.5 11.0 fusion.260
  281.5 11.7 fusion.261
  304.3 37.9 %multiply_convert_fusion.2 = (bf16[1024,3072]{1,0:T(8,128)(2,1)}, f32[1024,3072]{1,0:T(8,128)}, f32[1024,3072]{1,0:T(8,128)}) fusion(f32[3072]{0:T(1024)S(1)} %copy-done.112, bf16[768,3072]{1,0:T(8,128)(2,1)} %all-gather.11.cloned.1.call-done, f32[1024,768]{0,1:T(8,128)} %copy-done.15, f32[768]{0:T(1024)S(1)} %copy-done.118, f32[768]{0:T(1024)S(1)} %copy-done.94, ...), kind=kOutput, calls=%fused_computation.31 | convolution fusion | flops 5043388416 | bytes 39348224 | tf_op jit(solution)/shard_map/dot_general | solution.py:14
  342.2 19.8 %convert_reduce_fusion = (f32[3072]{0:T(1024)}, bf16[1024,3072]{1,0:T(8,128)(2,1)}) fusion(f32[1024,3072]{1,0:T(8,128)} %get-tuple-element.477, bf16[3072,768]{1,0:T(8,128)(2,1)} %all-gather.13.cloned.1.call-done, f32[1024,3072]{1,0:T(8,128)} %get-tuple-element.487, f32[3072]{0:T(1024)S(1)} %copy-done.112, f32[1,1024,768]{1,2,0:T(8,128)} %copy.135), kind=kOutput, calls=%fused_computation.29 | convolution fusion | flops 4885312512 | bytes 39346176 | tf_op jit(solution)/shard_map/dot_general | solution.py:24
  362.0 9.7 fusion.141
  387.8 189.1 %while.6 = (s32[]{:T(128)}, f32[1024,12,64]{0,2,1:T(8,128)}, f32[1024,12,64]{0,2,1:T(8,128)}, bf16[2,512,768]{2,1,0:T(8,128)(2,1)}, s32[2]{0:T(128)S(1)}, /*inde...) while((s32[]{:T(128)}, f32[1024,12,64]{0,2,1:T(8,128)}, ...), condition=%wide.region_22.23_spmd.clone, body=%wide.region_20.22_spmd.clone.sunk | while | flops 4086294528 | bytes 233742656 | solution.py:137
  394.9 11.9 fusion.272
  406.8 12.4 bitcast_add_fusion.8
  419.2 18.1 multiply_reduce_fusion.13
  437.3 21.4 %multiply_convert_fusion.7 = bf16[12,512,1024]{2,1,0:T(8,128)(2,1)} fusion(f32[12,512,1024]{2,1,0:T(8,128)} %get-tuple-element.629, f32[12,512,1024]{2,1,0:T(8,128)} %fusion.272, f32[12,512]{1,0:T(8,128)S(1)} %get-tuple-element.630, f32[12,512]{1,0:T(8,128)S(1)} %dynamic-slice_bitcast_fusion.2), kind=kLoop, calls=%fused_computation.8.clone.1 | loop fusion | flops 25165824 | bytes 62963712 | tf_op jit(solution)/shard_map/while/body/eval_jaxpr/convert_element_type | solution.py:123
  458.8 9.8 fusion.273
  468.6 8.6 bitcast_add_fusion.7
  488.5 11.5 fusion.272
  500.1 13.2 bitcast_add_fusion.8
  513.2 18.1 multiply_reduce_fusion.13
  531.3 21.4 %multiply_convert_fusion.7 = bf16[12,512,1024]{2,1,0:T(8,128)(2,1)} fusion(f32[12,512,1024]{2,1,0:T(8,128)} %get-tuple-element.629, f32[12,512,1024]{2,1,0:T(8,128)} %fusion.272, f32[12,512]{1,0:T(8,128)S(1)} %get-tuple-element.630, f32[12,512]{1,0:T(8,128)S(1)} %dynamic-slice_bitcast_fusion.2), kind=kLoop, calls=%fused_computation.8.clone.1 | loop fusion | flops 25165824 | bytes 62963712 | tf_op jit(solution)/shard_map/while/body/eval_jaxpr/convert_element_type | solution.py:123
  552.7 9.8 fusion.273
  562.5 9.4 bitcast_add_fusion.7
  640.0 5.3 fusion.9
  645.4 9.5 fusion.70
  657.8 17.5 multiply_convert_fusion.4
  675.3 10.6 convert_reduce_fusion.1
  696.4 12.4 convert_reduce_fusion.3
  708.8 18.0 multiply_reduce_fusion.1
  726.8 14.8 multiply_convert_fusion.1
  753.6 7.6 convert_reduce_fusion.10
  761.3 6.1 multiply_reduce_fusion.2
  784.5 10.5 fusion.109
  808.0 10.4 fusion.142
  819.7 7.2 fusion.107
  828.2 8.1 fusion.145
  861.7 10.4 add_bitcast_fusion.2
  884.3 5.0 add_bitcast_fusion
  892.7 13.4 all-reduce.12.cloned.1.call-done
  912.7 136.5 %reduce-scatter.11.cloned.1.call-done = f32[24,3072]{1,0:T(8,128)} async-done(((f32[768,3072]{1,0:T(8,128)}), f32[24,3072]{1,0:T(8,128)}) %reduce-scatter.11.cloned.1.call-update) | async-done | bytes 294928 | tf_op jit(solution)/shard_map/reduce_scatter | solution.py:404
  1049.1 142.2 %reduce-scatter.9.cloned.1.call-done = f32[4,24,768]{2,1,0:T(8,128)} async-done(((f32[4,768,768]{2,1,0:T(8,128)}), f32[4,24,768]{2,1,0:T(8,128)}) %reduce-scatter.9.cloned.1.call-update) | async-done | bytes 294928 | tf_op jit(solution)/shard_map/reduce_scatter | solution.py:409
  1191.4 140.9 %reduce-scatter.13.cloned.1.call-done = f32[96,768]{1,0:T(8,128)} async-done(((f32[3072,768]{1,0:T(8,128)}), f32[96,768]{1,0:T(8,128)}) %reduce-scatter.13.cloned.1.call-update) | async-done | bytes 294928 | tf_op jit(solution)/shard_map/reduce_scatter | solution.py:405
  1332.3 142.3 %reduce-scatter.17.cloned.1.call-done = f32[24,3072]{1,0:T(8,128)} async-done(((f32[768,3072]{1,0:T(8,128)}), f32[24,3072]{1,0:T(8,128)}) %reduce-scatter.17.cloned.1.call-update) | async-done | bytes 294928 | tf_op jit(solution)/shard_map/reduce_scatter | solution.py:393
  1474.6 140.8 %reduce-scatter.19.cloned.1.call-done = f32[96,768]{1,0:T(8,128)} async-done(((f32[3072,768]{1,0:T(8,128)}), f32[96,768]{1,0:T(8,128)}) %reduce-scatter.19.cloned.1.call-update) | async-done | bytes 294928 | tf_op jit(solution)/shard_map/reduce_scatter | solution.py:394
  1615.4 212.3 %reduce-scatter.15.cloned.1.call-done = f32[8,24,768]{2,1,0:T(8,128)} async-done(((f32[8,768,768]{2,1,0:T(8,128)}), f32[8,24,768]{2,1,0:T(8,128)}) %reduce-scatter.15.cloned.1.call-update) | async-done | bytes 589840 | tf_op jit(solution)/shard_map/reduce_scatter | solution.py:399
  (524 shorter events, 258.7 us)
Async XLA Ops:
  7.2 623.0 %copy-start = (bf16[1,1024,768]{2,1,0:T(8,128)(2,1)S(1)}, bf16[1,1024,768]{2,1,0:T(8,128)(2,1)}, u32[]{:S(2)}) copy-start(bf16[1,1024,768]{2,1,0:T(8,128)(2,1)} %param.23) | copy-start | bytes 4718596
  7.2 8.9 copy-start.134
  7.2 8.9 copy-start.135
  7.2 8.9 copy-start.136
  7.2 8.9 copy-start.121
  7.3 8.9 copy-start.31
  7.3 10.1 copy-start.114
  7.3 196.0 %all-gather.9.cloned.1.call-start = ((), (), s32[]{:S(2)}) async-start(), calls=%async_computation.6 | async-start | bytes 4866048 | tf_op jit(solution)/shard_map/all_gather | solution.py:354
  9.1 295.1 %all-gather.11.cloned.1.call-start = ((), (), s32[]{:S(2)}) async-start(), calls=%async_computation.7 | async-start | bytes 4866048 | tf_op jit(solution)/shard_map/all_gather | solution.py:355
  10.8 185.2 %copy-start.113 = (s32[1,448]{1,0:T(1,128)S(1)}, s32[1,448]{1,0:T(1,128)}, u32[]{:S(2)}) copy-start(s32[1,448]{1,0:T(1,128)} %param.24) | copy-start | bytes 5380
  10.9 331.3 %all-gather.13.cloned.1.call-start = ((), (), s32[]{:S(2)}) async-start(), calls=%async_computation.8 | async-start | bytes 4866048 | tf_op jit(solution)/shard_map/all_gather | solution.py:356
  12.6 586.5 %all-gather.15.cloned.1.call-start = ((), (), s32[]{:S(2)}) async-start(), calls=%async_computation.9 | async-start | bytes 9732096 | tf_op jit(solution)/shard_map/all_gather | solution.py:363
  14.5 643.3 %all-gather.17.cloned.1.call-start = ((), (), s32[]{:S(2)}) async-start(), calls=%async_computation.10 | async-start | bytes 4866048 | tf_op jit(solution)/shard_map/all_gather | solution.py:364
  15.2 660.1 %all-gather.19.cloned.1.call-start = ((), (), s32[]{:S(2)}) async-start(), calls=%async_computation.11 | async-start | bytes 4866048 | tf_op jit(solution)/shard_map/all_gather | solution.py:365
  16.0 890.1 %all-reduce.12.cloned.1.call-start = ((), (), s32[]{:S(2)}) async-start(), calls=%async_computation.18 | async-start | bytes 204800
  16.4 179.7 %copy-start.98 = (f32[448]{0:T(512)}, f32[448]{0:T(512)S(1)}, u32[]{:S(2)}) copy-start(f32[448]{0:T(512)S(1)} %broadcast_multiply_fusion.4) | copy-start | bytes 5380
  16.7 179.3 %copy-start.103 = (f32[448]{0:T(512)}, f32[448]{0:T(512)S(1)}, u32[]{:S(2)}) copy-start(f32[448]{0:T(512)S(1)} %fusion.71) | copy-start | bytes 5380
  130.0 83.5 %copy-start.80 = (f32[768]{0:T(1024)}, f32[768]{0:T(1024)S(1)}, u32[]{:S(2)}) copy-start(f32[768]{0:T(1024)S(1)} %get-tuple-element.415) | copy-start | bytes 9220
  130.0 83.5 %copy-start.116 = (f32[768]{0:T(1024)}, f32[768]{0:T(1024)S(1)}, u32[]{:S(2)}) copy-start(f32[768]{0:T(1024)S(1)} %get-tuple-element.414) | copy-start | bytes 9220
  199.2 14.2 copy-start.77
  199.7 13.8 copy-start.85
  217.5 80.7 %copy-start.120 = (f32[768]{0:T(1024)S(1)}, f32[768]{0:T(1024)}, u32[]{:S(2)}) copy-start(f32[768]{0:T(1024)} %get-tuple-element.411) | copy-start | bytes 9220
  230.1 11.0 copy-start.12
  270.5 11.0 copy-start.12
  302.2 78.1 %copy-start.83 = (f32[1024]{0:T(1024)}, f32[1024]{0:T(1024)S(1)}, u32[]{:S(2)}) copy-start(f32[1024]{0:T(1024)S(1)} %broadcast_multiply_fusion) | copy-start | bytes 12292
  304.2 76.1 %copy-start.96 = (f32[1024]{0:T(1024)}, f32[1024]{0:T(1024)S(1)}, u32[]{:S(2)}) copy-start(f32[1024]{0:T(1024)S(1)} %fusion.95) | copy-start | bytes 12292
  394.9 11.9 copy-start.5
  488.5 11.6 copy-start.5
  603.5 10.8 copy-start.38
  636.4 9.0 copy-start.1
  645.4 9.5 copy-start.26
  645.4 9.5 copy-start.107
  657.4 31.2 %copy-start.22 = (f32[448,768]{1,0:T(8,128)}, f32[448,768]{1,0:T(8,128)S(1)}, u32[]{:S(2)}) copy-start(f32[448,768]{1,0:T(8,128)S(1)} %get-tuple-element.495) | copy-start | bytes 4128772
  675.3 10.6 copy-start.133
  690.7 58.7 %copy-start.20 = (f32[448,768]{1,0:T(8,128)}, f32[448,768]{1,0:T(8,128)S(1)}, u32[]{:S(2)}) copy-start(f32[448,768]{1,0:T(8,128)S(1)} %get-tuple-element.459) | copy-start | bytes 4128772
  696.4 12.4 copy-start.40
  696.4 12.4 copy-start.62
  726.8 14.8 copy-start.43
  753.6 13.8 slice-start
  753.6 13.8 slice-start.1
  784.4 264.8 %reduce-scatter.11.cloned.1.call-start = ((), (), s32[]{:S(2)}) async-start(), calls=%async_computation.13 | async-start | bytes 9732096 | tf_op jit(solution)/shard_map/reduce_scatter | solution.py:404
  795.0 396.4 %reduce-scatter.9.cloned.1.call-start = ((), (), s32[]{:S(2)}) async-start(), calls=%async_computation.12 | async-start | bytes 9732096 | tf_op jit(solution)/shard_map/reduce_scatter | solution.py:409
  807.9 524.4 %reduce-scatter.13.cloned.1.call-start = ((), (), s32[]{:S(2)}) async-start(), calls=%async_computation.14 | async-start | bytes 9732096 | tf_op jit(solution)/shard_map/reduce_scatter | solution.py:405
  818.4 656.3 %reduce-scatter.17.cloned.1.call-start = ((), (), s32[]{:S(2)}) async-start(), calls=%async_computation.16 | async-start | bytes 9732096 | tf_op jit(solution)/shard_map/reduce_scatter | solution.py:393
  826.9 788.5 %reduce-scatter.19.cloned.1.call-start = ((), (), s32[]{:S(2)}) async-start(), calls=%async_computation.17 | async-start | bytes 9732096 | tf_op jit(solution)/shard_map/reduce_scatter | solution.py:394
  836.3 991.4 %reduce-scatter.15.cloned.1.call-start = ((), (), s32[]{:S(2)}) async-start(), calls=%async_computation.15 | async-start | bytes 19464192 | tf_op jit(solution)/shard_map/reduce_scatter | solution.py:399
  837.4 13.5 slice-start.3
  841.1 9.7 slice-start.4
  (115 other events, 395.2 us)
Sparse Core Ops, SparseCore 0:
  11.8 66.5 all-gather.8
  81.8 62.7 all-gather.10
  148.0 62.6 all-gather.12
  214.1 80.8 all-gather.14
  298.3 62.1 all-gather.16
  363.1 62.3 all-gather.18
  784.5 121.5 all-reduce.11
  912.6 136.5 reduce-scatter.10
  1056.6 134.7 reduce-scatter.8
  1197.7 134.5 reduce-scatter.12
  1339.8 134.7 reduce-scatter.16
  1480.9 134.4 reduce-scatter.18
  1623.5 204.1 reduce-scatter.14
where the time goes:
time: 1840 us; the launch traced here: 1830 us
  waiting for transfers between devices  929 us (50%)
  matrix products  493 us (27%)
  blocking collectives  175 us (10%)
  other arithmetic  129 us (7%)
  local copies, waits for them, and re-layouts  88.6 us (5%)
    reduce_scatter x1, waiting for transfers between devices, body(): lax.psum_scatter(dec_parts[0], ('fsdp', 'rep'), scatter_dimension=1, tile...  212 us
    reduce_scatter x1, waiting for transfers between devices, body(): lax.psum_scatter(dec_parts[1], ('fsdp', 'rep'), scatter_dimension=0, tile...  142 us
    reduce_scatter x1, waiting for transfers between devices, body(): lax.psum_scatter(enc_parts[0], ('fsdp', 'rep'), scatter_dimension=1, tile...  142 us
    reduce_scatter x1, waiting for transfers between devices, body(): lax.psum_scatter(enc_parts[2], ('fsdp', 'rep'), scatter_dimension=0, tile...  141 us
    reduce_scatter x1, waiting for transfers between devices, body(): lax.psum_scatter(dec_parts[2], ('fsdp', 'rep'), scatter_dimension=0, tile...  141 us
    reduce_scatter x1, waiting for transfers between devices, body(): lax.psum_scatter(enc_parts[1], ('fsdp', 'rep'), scatter_dimension=0, tile...  136 us
    dot_general x16, matrix products, matmul(): return jnp.dot(left, right, preferred_element_type=jnp.float32)  107 us
    dot_general x16, matrix products, right_product(): lax.dot_general(left, right, (((1,), (1,)), ((), ())), preferred_element_...  79.7 us
  transfers between devices with their start and end apart: 13, of which 7 were waited for; matrix products, arithmetic and copies ran while one was open for 32% of the time, Pallas kernels for 0%

commit v1 on v0

v1 whole, which is shorter than its diff:
```python
import functools

import jax
import jax.numpy as jnp
from jax import lax
from jax.experimental import pallas as pl
from jax.experimental.pallas import tpu as pltpu
from jax.sharding import PartitionSpec as P

HEADS = 12
epsilon = 1e-05
masked_score = -1e30
low = jnp.bfloat16
full = jnp.float32
MIB = 1024 * 1024


def dot_nn(left, right):
    return lax.dot_general(left, right, (((1,), (0,)), ((), ())), preferred_element_type=full)


def dot_nt(left, right):
    return lax.dot_general(left, right, (((1,), (1,)), ((), ())), preferred_element_type=full)


def dot_tn(left, right):
    return lax.dot_general(left, right, (((0,), (0,)), ((), ())), preferred_element_type=full)


def whole(shape):
    return pl.BlockSpec(shape, lambda *_: (0,) * len(shape), pipeline_mode=pl.Buffered(1))


def kept(shape):
    return pl.BlockSpec(shape, lambda *_: (0,) * len(shape))


def rows(count, width):
    return pl.BlockSpec((count, width), lambda i: (i, 0))


def shape_of(shape, kind):
    return jax.ShapeDtypeStruct(shape, kind)


def call(kernel, grid, in_specs, out_specs, out_shape, args, flops, scratch=(), exps=0, limit=48):
    moved = sum(a.size * a.dtype.itemsize for a in args)
    moved += sum(s.size * s.dtype.itemsize for s in out_shape)
    return pl.pallas_call(
        kernel,
        grid=grid,
        in_specs=in_specs,
        out_specs=out_specs,
        out_shape=out_shape,
        scratch_shapes=list(scratch),
        cost_estimate=pl.CostEstimate(
            flops=int(flops), bytes_accessed=int(moved), transcendentals=int(exps)
        ),
        compiler_params=pltpu.CompilerParams(vmem_limit_bytes=limit * MIB),
    )(*args)


def block_of(count):
    return 256 if count % 256 == 0 else count // 2 if (count // 2) % 16 == 0 else count


def spread_of(inputs):
    center = inputs - jnp.mean(inputs, -1, keepdims=True)
    rate = lax.rsqrt(jnp.mean(center * center, -1, keepdims=True) + epsilon)
    return center * rate, rate


def norm_pull(unit, rate, gain, upstream):
    a = upstream * gain
    along = jnp.mean(a * unit, -1, keepdims=True)
    return rate * (a - jnp.mean(a, -1, keepdims=True) - unit * along)


def add_row(ref, row, block):
    ref[pl.ds(row, 1), :] += jnp.sum(block.astype(full), 0, keepdims=True)


def clear_at_start(*refs):
    @pl.when(pl.program_id(0) == 0)
    def _():
        for ref in refs:
            ref[...] = jnp.zeros_like(ref)


def norm_project_kernel(scale, x_ref, vec_ref, wq_ref, wk_ref, wv_ref, n_ref, q_ref, k_ref, v_ref):
    unit, _ = spread_of(x_ref[...].astype(full))
    n = (unit * vec_ref[0:1, :] + vec_ref[1:2, :]).astype(low)
    n_ref[...] = n
    q_ref[...] = ((dot_nn(n, wq_ref[...]) + vec_ref[2:3, :]) * scale).astype(low)
    k_ref[...] = dot_nn(n, wk_ref[...]).astype(low)
    v_ref[...] = (dot_nn(n, wv_ref[...]) + vec_ref[3:4, :]).astype(low)


def norm_project(x, vecs, wq, wk, wv):
    count, width = x.shape
    step = block_of(count)
    out = shape_of((count, width), low)
    return call(
        functools.partial(norm_project_kernel, (width // HEADS) ** -0.5),
        (count // step,),
        [rows(step, width), whole(vecs.shape)] + [whole((width, width))] * 3,
        [rows(step, width)] * 4,
        [out] * 4,
        (x, vecs, wq, wk, wv),
        6 * count * width * width,
    )


def allowed_bias(seg_a, seg_b, a_axis):
    shape = (seg_a.size, seg_b.size)
    first = lax.broadcasted_iota(jnp.int32, shape, 0)
    second = lax.broadcasted_iota(jnp.int32, shape, 1)
    later = second <= first if a_axis == 0 else first <= second
    return jnp.where((seg_a == seg_b) & later, 0.0, masked_score).astype(full)


def attend_kernel(step, masked, *refs):
    if masked:
        q_ref, k_ref, v_ref, col_ref, row_ref, o_ref, sum_ref, hold, bias = refs
    else:
        q_ref, k_ref, v_ref, o_ref, sum_ref, hold = refs
    pair = pl.program_id(0)
    count = q_ref.shape[0]
    lane = lax.broadcasted_iota(jnp.int32, (1, 128), 1)
    k, v = k_ref[...], v_ref[...]

    @pl.when(pair == 0)
    def _():
        hold[...] = jnp.zeros_like(hold)
        if masked:
            bias[...] = allowed_bias(col_ref[...], row_ref[...], 0)

    def one(index, carry):
        start = pl.multiple_of(index * step, step)
        block = q_ref[pl.ds(start, step), :]
        outs = []
        sums = hold[pl.ds(start, step), :]
        for h in range(2):
            mine = (lane < 64) == (h == 0)
            s = dot_nt(jnp.where(mine, block, jnp.zeros_like(block)), k)
            if masked:
                s = s + bias[pl.ds(start, step), :]
            top = jnp.max(s, -1, keepdims=True)
            e = jnp.exp(s - top)
            total = jnp.sum(e, -1, keepdims=True)
            outs.append(dot_nn(e.astype(low), v) / total)
            sums = jnp.where(lane == 2 * pair + h, top + jnp.log(total), sums)
        o_ref[pl.ds(start, step), :] = jnp.where(lane < 64, outs[0], outs[1]).astype(low)
        hold[pl.ds(start, step), :] = sums
        return carry

    lax.fori_loop(0, count // step, one, 0)

    @pl.when(pair == pl.num_programs(0) - 1)
    def _():
        sum_ref[...] = hold[...].T[:16, :]


def attend(q, k, v, seg=None):
    count, width = q.shape
    keys = k.shape[0]
    step = block_of(count)
    pairs = width // 128
    column = lambda n: pl.BlockSpec((n, 128), lambda j: (0, j))
    args, specs = [q, k, v], [column(count), column(keys), column(keys)]
    scratch = [pltpu.VMEM((count, 128), full)]
    if seg is not None:
        args += [seg.reshape(count, 1), seg.reshape(1, count)]
        specs += [whole((count, 1)), whole((1, count))]
        scratch.append(pltpu.VMEM((count, count), full))
    return call(
        functools.partial(attend_kernel, step, seg is not None),
        (pairs,),
        specs,
        [column(count), kept((16, count))],
        [shape_of((count, width), low), shape_of((16, count), full)],
        args,
        8 * 2 * count * keys * width,
        scratch,
        HEADS * count * keys,
    )


def attend_back_kernel(step, masked, scale, *refs):
    if masked:
        q_ref, k_ref, v_ref, o_ref, g_ref, sum_ref, col_ref, row_ref, gq_ref, gk_ref, gv_ref, acc_k, acc_v, dots, bias = refs
    else:
        q_ref, k_ref, v_ref, o_ref, g_ref, sum_ref, gq_ref, gk_ref, gv_ref, acc_k, acc_v, dots = refs
    pair = pl.program_id(0)
    count = q_ref.shape[0]
    lane = lax.broadcasted_iota(jnp.int32, (1, 128), 1)
    k, v = k_ref[...], v_ref[...]
    if masked:

        @pl.when(pair == 0)
        def _():
            bias[...] = allowed_bias(col_ref[...], row_ref[...], 1)

    acc_k[...] = jnp.zeros_like(acc_k)
    acc_v[...] = jnp.zeros_like(acc_v)

    def one(index, carry):
        start = pl.multiple_of(index * step, step)
        span = pl.ds(start, step)
        q, g = q_ref[span, :], g_ref[span, :]
        both = (g.astype(full) * o_ref[span, :].astype(full)).T
        gqs = []
        for h in range(2):
            mine = (lane < 64) == (h == 0)
            qh = jnp.where(mine, q, jnp.zeros_like(q))
            gh = jnp.where(mine, g, jnp.zeros_like(g))
            top = sum_ref[pl.ds(2 * pair + h, 1), span]
            s = dot_nt(k, qh)
            if masked:
                s = s + bias[:, span]
            p = jnp.exp(s - top)
            away = dot_nt(v, gh) - jnp.sum(both[64 * h : 64 * h + 64, :], 0, keepdims=True)
            gs = (p * away).astype(low)
            acc_v[...] += dot_nn(p.astype(low), gh)
            acc_k[...] += dot_nn(gs, qh)
            gqs.append(dot_tn(gs, k))
        gq_ref[span, :] = (jnp.where(lane < 64, gqs[0], gqs[1]) * scale).astype(low)
        return carry

    if count == step:
        one(0, 0)
    else:
        lax.fori_loop(0, count // step, one, 0)
    gk_ref[...] = acc_k[...].astype(low)
    gv_ref[...] = acc_v[...].astype(low)


def attend_back(q, k, v, o, g, sums, seg=None):
    count, width = q.shape
    keys = k.shape[0]
    step = 256 if count % 256 == 0 else count
    pairs = width // 128
    column = lambda n: pl.BlockSpec((n, 128), lambda j: (0, j))
    args = [q, k, v, o, g, sums]
    specs = [column(count), column(keys), column(keys), column(count), column(count), whole((16, count))]
    scratch = [pltpu.VMEM((keys, 128), full), pltpu.VMEM((keys, 128), full), pltpu.VMEM((8, 128), full)]
    if seg is not None:
        args += [seg.reshape(count, 1), seg.reshape(1, count)]
        specs += [whole((count, 1)), whole((1, count))]
        scratch.append(pltpu.VMEM((count, count), full))
    return call(
        functools.partial(attend_back_kernel, step, seg is not None, (width // HEADS) ** -0.5),
        (pairs,),
        specs,
        [column(count), column(keys), column(keys)],
        [shape_of((count, width), low), shape_of((keys, width), low), shape_of((keys, width), low)],
        args,
        20 * 2 * count * keys * width,
        scratch,
        HEADS * count * keys,
    )


def feed_kernel(
    chunk,
    x_ref, o_ref, up_ref, vec_ref, bias_ref, wo_ref, wu_ref, wd_ref,
    out_ref, n_ref, hid_ref, gpre_ref, gr_ref, gmid_ref, grm_ref, go_ref, sums_ref, gbias_ref,
):
    clear_at_start(sums_ref, gbias_ref)
    mid = x_ref[...].astype(full) + dot_nn(o_ref[...], wo_ref[...]) + vec_ref[0:1, :]
    unit, rate = spread_of(mid)
    n = (unit * vec_ref[1:2, :] + vec_ref[2:3, :]).astype(low)
    n_ref[...] = n
    upstream = up_ref[...]
    gr = upstream.astype(low)
    gr_ref[...] = gr
    add_row(sums_ref, 0, gr)
    total = gn = None
    for first in range(0, wu_ref.shape[1], chunk):
        cut = slice(first, first + chunk)
        pre = dot_nn(n, wu_ref[:, cut]) + bias_ref[:, cut]
        half = 0.5 + 0.5 * lax.erf(pre * 0.7071067811865476)
        hid = (pre * half).astype(low)
        slope = half + pre * (0.3989422804014327 * jnp.exp(-0.5 * pre * pre))
        gpre = (dot_nt(gr, wd_ref[cut, :]) * slope).astype(low)
        hid_ref[:, cut] = hid
        gpre_ref[:, cut] = gpre
        gbias_ref[:, cut] += jnp.sum(gpre.astype(full), 0, keepdims=True)
        one, two = dot_nn(hid, wd_ref[cut, :]), dot_nt(gpre, wu_ref[:, cut])
        total = one if total is None else total + one
        gn = two if gn is None else gn + two
    out_ref[...] = mid + total + vec_ref[3:4, :]
    add_row(sums_ref, 1, gn * unit)
    add_row(sums_ref, 2, gn)
    gmid = upstream + norm_pull(unit, rate, vec_ref[1:2, :], gn)
    gmid_ref[...] = gmid
    grm = gmid.astype(low)
    grm_ref[...] = grm
    add_row(sums_ref, 3, grm)
    go_ref[...] = dot_nt(grm, wo_ref[...]).astype(low)


def feed(x, o, upstream, vecs, bias, wo, wu, wd, chunk=768):
    count, width = x.shape
    ff = wu.shape[1]
    step = block_of(count)
    wide, thin = rows(step, ff), rows(step, width)
    return call(
        functools.partial(feed_kernel, chunk),
        (count // step,),
        [thin, thin, thin, whole(vecs.shape), whole(bias.shape), whole(wo.shape), whole(wu.shape), whole(wd.shape)],
        [thin, thin, wide, wide, thin, thin, thin, thin, kept((8, width)), kept((1, ff))],
        [
            shape_of((count, width), full),
            shape_of((count, width), low),
            shape_of((count, ff), low),
            shape_of((count, ff), low),
            shape_of((count, width), low),
            shape_of((count, width), full),
            shape_of((count, width), low),
            shape_of((count, width), low),
            shape_of((8, width), full),
            shape_of((1, ff), full),
        ],
        (x, o, upstream, vecs, bias, wo, wu, wd),
        4 * count * width * width + 8 * count * width * ff,
        exps=2 * count * ff,
        limit=56,
    )


def project_back_kernel(x_ref, up_ref, gq_ref, gk_ref, gv_ref, vec_ref, wq_ref, wk_ref, wv_ref, gx_ref, sums_ref):
    clear_at_start(sums_ref)
    gq, gk, gv = gq_ref[...], gk_ref[...], gv_ref[...]
    gn = dot_nt(gq, wq_ref[...]) + dot_nt(gk, wk_ref[...]) + dot_nt(gv, wv_ref[...])
    unit, rate = spread_of(x_ref[...].astype(full))
    add_row(sums_ref, 0, gn * unit)
    add_row(sums_ref, 1, gn)
    add_row(sums_ref, 2, gq)
    add_row(sums_ref, 3, gv)
    gx_ref[...] = up_ref[...] + norm_pull(unit, rate, vec_ref[0:1, :], gn)


def project_back(x, upstream, gq, gk, gv, vecs, wq, wk, wv):
    count, width = x.shape
    step = block_of(count)
    thin = rows(step, width)
    return call(
        project_back_kernel,
        (count // step,),
        [thin] * 5 + [whole(vecs.shape)] + [whole((width, width))] * 3,
        [thin, kept((8, width))],
        [shape_of((count, width), full), shape_of((8, width), full)],
        (x, upstream, gq, gk, gv, vecs, wq, wk, wv),
        6 * count * width * width,
    )


def bridge_kernel(scale, x_ref, o_ref, vec_ref, wo_ref, wq_ref, mid_ref, n_ref, q_ref):
    mid = x_ref[...].astype(full) + dot_nn(o_ref[...], wo_ref[...]) + vec_ref[0:1, :]
    mid_ref[...] = mid
    unit, _ = spread_of(mid)
    n = (unit * vec_ref[1:2, :] + vec_ref[2:3, :]).astype(low)
    n_ref[...] = n
    q_ref[...] = ((dot_nn(n, wq_ref[...]) + vec_ref[3:4, :]) * scale).astype(low)


def bridge(x, o, vecs, wo, wq):
    count, width = x.shape
    step = block_of(count)
    thin = rows(step, width)
    return call(
        functools.partial(bridge_kernel, (width // HEADS) ** -0.5),
        (count // step,),
        [thin, thin, whole(vecs.shape), whole((width, width)), whole((width, width))],
        [thin] * 3,
        [shape_of((count, width), full), shape_of((count, width), low), shape_of((count, width), low)],
        (x, o, vecs, wo, wq),
        4 * count * width * width,
    )


def bridge_back_kernel(mid_ref, up_ref, gq_ref, vec_ref, wo_ref, wq_ref, g_ref, gr_ref, go_ref, sums_ref):
    clear_at_start(sums_ref)
    gq = gq_ref[...]
    gn = dot_nt(gq, wq_ref[...])
    unit, rate = spread_of(mid_ref[...])
    add_row(sums_ref, 0, gn * unit)
    add_row(sums_ref, 1, gn)
    add_row(sums_ref, 2, gq)
    g = up_ref[...] + norm_pull(unit, rate, vec_ref[1:2, :], gn)
    g_ref[...] = g
    gr = g.astype(low)
    gr_ref[...] = gr
    add_row(sums_ref, 3, gr)
    go_ref[...] = dot_nt(gr, wo_ref[...]).astype(low)


def bridge_back(mid, upstream, gq, vecs, wo, wq):
    count, width = mid.shape
    step = block_of(count)
    thin = rows(step, width)
    return call(
        bridge_back_kernel,
        (count // step,),
        [thin] * 3 + [whole(vecs.shape), whole((width, width)), whole((width, width))],
        [thin] * 3 + [kept((8, width))],
        [
            shape_of((count, width), full),
            shape_of((count, width), low),
            shape_of((count, width), low),
            shape_of((8, width), full),
        ],
        (mid, upstream, gq, vecs, wo, wq),
        4 * count * width * width,
    )


def memory_kernel(s_ref, vec_ref, wk_ref, wv_ref, k_ref, v_ref):
    s = s_ref[...]
    k_ref[...] = dot_nn(s, wk_ref[...]).astype(low)
    v_ref[...] = (dot_nn(s, wv_ref[...]) + vec_ref[0:1, :]).astype(low)


def memory_project(s, vecs, wk, wv):
    count, width = s.shape
    step = block_of(count)
    thin = rows(step, width)
    return call(
        memory_kernel,
        (count // step,),
        [thin, whole(vecs.shape), whole((width, width)), whole((width, width))],
        [thin] * 2,
        [shape_of((count, width), low)] * 2,
        (s, vecs, wk, wv),
        4 * count * width * width,
    )


def memory_back_kernel(gk_ref, gv_ref, wk_ref, wv_ref, g_ref, sums_ref):
    clear_at_start(sums_ref)
    gv = gv_ref[...]
    g_ref[...] = dot_nt(gk_ref[...], wk_ref[...]) + dot_nt(gv, wv_ref[...])
    add_row(sums_ref, 0, gv)


def memory_back(gk, gv, wk, wv):
    count, width = gk.shape
    step = block_of(count)
    thin = rows(step, width)
    return call(
        memory_back_kernel,
        (count // step,),
        [thin] * 2 + [whole((width, width))] * 2,
        [thin, kept((8, width))],
        [shape_of((count, width), full), shape_of((8, width), full)],
        (gk, gv, wk, wv),
        4 * count * width * width,
    )


def weight_grad(left, right):
    return dot_tn(left, right).astype(low)


def eight(*parts):
    table = jnp.concatenate([p.reshape(-1, p.shape[-1]) for p in parts], 0)
    return jnp.pad(table, ((0, 8 - table.shape[0]), (0, 0)))


def encoder(x, weights, upstream):
    wq, wk, wv, wo, wu, wd, vecs, up_bias = weights
    n1, q, k, v = norm_project(x, eight(vecs[0:4]), wq, wk, wv)
    o, sums = attend(q, k, v)
    out, n2, hid, gpre, gr, gmid, grm, go, feed_sums, gbias = feed(
        x, o, upstream, eight(vecs[4:8]), up_bias, wo, wu, wd
    )
    feed_grads = (weight_grad(n2, gpre), weight_grad(hid, gr))
    feed_grads, go = lax.optimization_barrier((feed_grads, go))
    gq, gk, gv = attend_back(q, k, v, o, go, sums)
    gx, first_sums = project_back(x, gmid, gq, gk, gv, eight(vecs[0:2]), wq, wk, wv)
    attn_grads = (
        weight_grad(n1, gq),
        weight_grad(n1, gk),
        weight_grad(n1, gv),
        weight_grad(o, grm),
    )
    vec_grad = jnp.concatenate([first_sums[0:4], feed_sums[3:4], feed_sums[1:3], feed_sums[0:1]], 0)
    return out, gx, attn_grads, feed_grads, vec_grad, gbias


def decoder(y, memory, seg, weights, upstream):
    wq, wk, wv, wo, cq, ck, cv, co, wu, wd, vecs, up_bias, down_bias = weights
    m1, q, k, v = norm_project(y, eight(vecs[0:4]), wq, wk, wv)
    o, sums = attend(q, k, v, seg)
    first, m2, q2 = bridge(y, o, eight(vecs[4:8]), wo, cq)
    k2, v2 = memory_project(memory, eight(vecs[8:9]), ck, cv)
    o2, sums2 = attend(q2, k2, v2)
    out, m3, hid, gpre, gr, gsecond, grs, go2, feed_sums, gbias = feed(
        first, o2, upstream, eight(vecs[9:12], down_bias), up_bias, co, wu, wd
    )
    feed_grads = (weight_grad(m3, gpre), weight_grad(hid, gr))
    feed_grads, go2 = lax.optimization_barrier((feed_grads, go2))
    gq2, gk2, gv2 = attend_back(q2, k2, v2, o2, go2, sums2)
    gmemory, memory_sums = memory_back(gk2, gv2, ck, cv)
    gfirst, grf, go, bridge_sums = bridge_back(first, gsecond, gq2, eight(vecs[4:8]), wo, cq)
    gq, gk, gv = attend_back(q, k, v, o, go, sums, seg)
    gy, first_sums = project_back(y, gfirst, gq, gk, gv, eight(vecs[0:2]), wq, wk, wv)
    attn_grads = (
        weight_grad(m1, gq),
        weight_grad(m1, gk),
        weight_grad(m1, gv),
        weight_grad(o, grf),
        weight_grad(m2, gq2),
        weight_grad(memory, gk2),
        weight_grad(memory, gv2),
        weight_grad(o2, grs),
    )
    vec_grad = jnp.concatenate(
        [
            first_sums[0:4],
            bridge_sums[3:4],
            bridge_sums[0:3],
            memory_sums[0:1],
            feed_sums[3:4],
            feed_sums[1:3],
        ],
        0,
    )
    return out, gy, gmemory, attn_grads, feed_grads, vec_grad, gbias, feed_sums[0:1]


def parts_of(size):
    even = [list(range(k, size, 2)) for k in range(2)]
    swap = [(k, k ^ 1) for k in range(size)]
    return even, swap


def gather_rows(packed, fsdp):
    even, swap = parts_of(fsdp)
    rows, width = packed.shape
    lines = lax.all_gather(packed, "rep", axis=0, tiled=False)
    mine = lax.all_gather(lines, "fsdp", axis=0, tiled=False, axis_index_groups=even)
    other = lax.ppermute(mine, "fsdp", swap)
    first = lax.axis_index("fsdp") % 2 == 0
    whole = jnp.stack([jnp.where(first, mine, other), jnp.where(first, other, mine)], 1)
    return whole.reshape(-1, rows, width)


def scatter_rows(parts, fsdp):
    even, swap = parts_of(fsdp)
    shards, rows, width = parts.shape
    laid = parts.reshape(fsdp // 2, 2, shards // fsdp, rows, width)
    core = lax.axis_index("fsdp") % 2
    theirs = lax.dynamic_index_in_dim(laid, 1 - core, 1, keepdims=False)
    ours = lax.dynamic_index_in_dim(laid, core, 1, keepdims=False)
    one = ours + lax.ppermute(theirs, "fsdp", swap)
    two = lax.psum_scatter(one, "fsdp", scatter_dimension=0, tiled=False, axis_index_groups=even)
    return lax.psum_scatter(two, "rep", scatter_dimension=0, tiled=False)


def slots_of(whole, first, count, own):
    shards, _, width = whole.shape
    part = whole[:, first * own : (first + count) * own].reshape(shards, count, own, width)
    return part.transpose(1, 0, 2, 3).reshape(count, shards * own, width)


def rows_of(slots, shards):
    count, total, width = slots.shape
    own = total // shards
    part = slots.astype(jnp.bfloat16).reshape(count, shards, own, width)
    return part.transpose(1, 0, 2, 3).reshape(shards, count * own, width)


def columns_to_slots(up):
    rows, columns = up.shape
    return up.reshape(rows, columns // 768, 768).transpose(1, 0, 2)


def body(
    fsdp,
    rep,
    frames,
    tokens,
    memory,
    segment_ids,
    enc_attn,
    enc_up,
    enc_down,
    enc_vec,
    enc_up_bias,
    dec_attn,
    dec_up,
    dec_down,
    dec_vec,
    dec_up_bias,
    dec_down_bias,
    enc_out_grad,
    dec_out_grad,
):
    shards = fsdp * rep
    own = enc_attn.shape[1]
    width = enc_attn.shape[2]
    ff = enc_up.shape[1]
    wide = ff // width

    def pack(attn, up, down):
        low = [attn.astype(jnp.bfloat16).reshape(-1, width)]
        if up is not None:
            low.append(columns_to_slots(up.astype(jnp.bfloat16)).reshape(-1, width))
            low.append(down.astype(jnp.bfloat16))
        return jnp.concatenate(low, 0)

    def unpack(whole, slots):
        attn = slots_of(whole, 0, slots, own)
        up = slots_of(whole, slots, wide, own).transpose(1, 0, 2).reshape(width, ff)
        down = whole[:, (slots + wide) * own :].reshape(ff, width)
        return attn, up, down

    small = jnp.concatenate(
        [
            enc_vec.reshape(-1),
            dec_vec.reshape(-1),
            enc_up_bias,
            dec_up_bias,
            dec_down_bias,
        ]
    ).astype(jnp.bfloat16)
    small_all = lax.all_gather(small, ("fsdp", "rep"), axis=0, tiled=False)
    cuts = [8 * own, 12 * own, wide * own, wide * own, own]
    edges = [sum(cuts[:k]) for k in range(6)]
    piece = [small_all[:, edges[k] : edges[k + 1]] for k in range(5)]
    enc_vec_w = piece[0].reshape(shards, 8, own).transpose(1, 0, 2).reshape(8, width)
    dec_vec_w = piece[1].reshape(shards, 12, own).transpose(1, 0, 2).reshape(12, width)
    enc_bias_w = piece[2].reshape(ff)
    dec_bias_w = piece[3].reshape(ff)
    dec_down_bias_w = piece[4].reshape(width)

    enc_whole = gather_rows(pack(enc_attn, enc_up, enc_down), fsdp)
    dec_whole = gather_rows(pack(dec_attn, dec_up, dec_down), fsdp)
    enc_attn_w, enc_up_w, enc_down_w = unpack(enc_whole, 4)
    dec_attn_w, dec_up_w, dec_down_w = unpack(dec_whole, 8)
    enc_weights = (enc_attn_w, enc_up_w, enc_down_w, enc_vec_w, enc_bias_w)
    dec_weights = (dec_attn_w, dec_up_w, dec_down_w, dec_vec_w, dec_bias_w, dec_down_bias_w)

    enc_set = tuple(enc_attn_w[k] for k in range(4)) + (
        enc_up_w,
        enc_down_w,
        enc_vec_w.astype(full),
        enc_bias_w.astype(full)[None],
    )
    dec_set = tuple(dec_attn_w[k] for k in range(8)) + (
        dec_up_w,
        dec_down_w,
        dec_vec_w.astype(full),
        dec_bias_w.astype(full)[None],
        dec_down_bias_w.astype(full)[None],
    )

    def reduce_feed(grads):
        up_rows = rows_of(columns_to_slots(grads[0]), shards)
        down_rows = grads[1].reshape(shards, -1, width)
        mine = scatter_rows(jnp.concatenate([up_rows, down_rows], 1), fsdp).astype(full)
        up_mine = mine[: wide * own].reshape(wide, own, width).transpose(1, 0, 2).reshape(own, ff)
        return up_mine, mine[wide * own :]

    def reduce_attn(grads):
        parts = jnp.concatenate([g.reshape(shards, own, width) for g in grads], 1)
        return scatter_rows(parts, fsdp).astype(full).reshape(-1, own, width)

    enc_result, frames_grad, enc_attn_g, enc_feed_g, enc_vec_g, enc_bias_g = encoder(
        frames[0], enc_set, enc_out_grad[0]
    )
    enc_up_grad, enc_down_grad = reduce_feed(enc_feed_g)
    enc_attn_grad = reduce_attn(enc_attn_g)
    token_rows, frames_grad = lax.optimization_barrier((tokens[0], frames_grad))
    (
        dec_result,
        tokens_grad,
        memory_grad,
        dec_attn_g,
        dec_feed_g,
        dec_vec_g,
        dec_bias_g,
        dec_down_bias_g,
    ) = decoder(token_rows, memory[0], segment_ids[0], dec_set, dec_out_grad[0])
    dec_up_grad, dec_down_grad = reduce_feed(dec_feed_g)
    dec_attn_grad = reduce_attn(dec_attn_g)

    def by_owner(table):
        count = table.shape[0]
        return table.reshape(count, shards, -1).transpose(1, 0, 2).reshape(shards, -1)

    small_grad = jnp.concatenate(
        [
            by_owner(enc_vec_g),
            by_owner(dec_vec_g),
            by_owner(enc_bias_g),
            by_owner(dec_bias_g),
            by_owner(dec_down_bias_g),
        ],
        1,
    )
    spare = -small_grad.shape[1] % 1024
    small_grad = jnp.pad(small_grad, ((0, 0), (0, spare))).reshape(shards, -1, 128)
    small_mine = lax.psum_scatter(
        small_grad, ("fsdp", "rep"), scatter_dimension=0, tiled=False
    ).reshape(-1)
    take = [small_mine[edges[k] : edges[k + 1]] for k in range(5)]
    return (
        enc_result[None],
        dec_result[None],
        frames_grad[None],
        tokens_grad[None],
        memory_grad[None],
        enc_attn_grad,
        enc_up_grad,
        enc_down_grad,
        take[0].reshape(8, own),
        take[2],
        dec_attn_grad,
        dec_up_grad,
        dec_down_grad,
        take[1].reshape(12, own),
        take[3],
        take[4],
    )


def solution(mesh):
    placed = (
        P(("fsdp", "rep"), None, None),
        P(("fsdp", "rep"), None, None),
        P(("fsdp", "rep"), None, None),
        P(("fsdp", "rep"), None),
        P(None, ("fsdp", "rep"), None),
        P(("fsdp", "rep"), None),
        P(("fsdp", "rep"), None),
        P(None, ("fsdp", "rep")),
        P(("fsdp", "rep")),
        P(None, ("fsdp", "rep"), None),
        P(("fsdp", "rep"), None),
        P(("fsdp", "rep"), None),
        P(None, ("fsdp", "rep")),
        P(("fsdp", "rep")),
        P(("fsdp", "rep")),
        P(("fsdp", "rep"), None, None),
        P(("fsdp", "rep"), None, None),
    )
    return jax.shard_map(
        functools.partial(body, mesh.shape["fsdp"], mesh.shape["rep"]),
        mesh=mesh,
        in_specs=placed,
        out_specs=(
            P(("fsdp", "rep"), None, None),
            P(("fsdp", "rep"), None, None),
            P(("fsdp", "rep"), None, None),
            P(("fsdp", "rep"), None, None),
            P(("fsdp", "rep"), None, None),
            P(None, ("fsdp", "rep"), None),
            P(("fsdp", "rep"), None),
            P(("fsdp", "rep"), None),
            P(None, ("fsdp", "rep")),
            P(("fsdp", "rep")),
            P(None, ("fsdp", "rep"), None),
            P(("fsdp", "rep"), None),
            P(("fsdp", "rep"), None),
            P(None, ("fsdp", "rep")),
            P(("fsdp", "rep")),
            P(("fsdp", "rep")),
        ),
        check_vma=False,
    )
```

time: 1840 us -> 1050 us (0.57)
  waiting for transfers between devices: 929 us -> 467 us
  matrix products: 493 us -> 41.3 us
  Pallas kernels: 0 us -> 221 us
  blocking collectives: 175 us -> 69.6 us
  local copies, waits for them, and re-layouts: 88.6 us -> 147 us
  other arithmetic: 129 us -> 76.1 us
    reduce_scatter x6 -> x4, waiting for transfers between devices: 915 us -> 102 us  [scatter_rows(): return lax.psum_scatter(two, 'rep', scatter_dimension=0, tiled=False)]
    dot_general x74 -> x16, matrix products: 493 us -> 41.3 us  [dot_tn(): lax.dot_general(left, right, (((0,), (0,)), ((), ())), preferred_element_...]
    pallas_call x0 -> x16, Pallas kernels: none -> 221 us  [call(): pl.pallas_call(kernel, grid=grid, in_specs=in_specs, out_specs=out_specs,...]
    all_gather x6 -> x4, waiting for transfers between devices: 0.05 us -> 194 us  [the longest x2 102 us: gather_rows(): lax.all_gather(lines, 'fsdp', axis=0, tiled=False, axis_index_groups=even)]
    unnamed x14 -> x18, waiting for transfers between devices: 13.6 us -> 164 us
    all_gather x2 -> x1, blocking collectives: 132 us -> 69.6 us  [body(): small_all = lax.all_gather(small, ('fsdp', 'rep'), axis=0, tiled=False)]
    convert_element_type x17 -> x14, other arithmetic: 72 us -> 12.6 us  [the longest x2 3.46 us: reduce_attn(): return scatter_rows(parts, fsdp).astype(full).reshape(-1, own, width)]
    reduce_sum x23 -> x0, other arithmetic: 49.5 us -> none  [the longest x4 29.6 us: one_block(): row_sum = jnp.sum(exp_scores, -1, keepdims=True)]
  transfers between devices with their start and end apart: 13 -> 19, of which waited for: 7 -> 11; matrix products, arithmetic and copies ran while one was open for 32% -> 21% of each run, Pallas kernels for 0% -> 21%
where the time goes in v1:
time: 1050 us; the launch traced here: 1040 us
  waiting for transfers between devices  467 us (44%)
  Pallas kernels  221 us (21%)
  local copies, waits for them, and re-layouts  147 us (14%)
  other arithmetic  76.1 us (7%)
  blocking collectives  69.6 us (7%)
  matrix products  41.3 us (4%)
  between operations  15.5 us (1%)
    pallas_call x16, Pallas kernels, call(): pl.pallas_call(kernel, grid=grid, in_specs=in_specs, out_specs=out_specs,...  221 us
    unnamed x18, waiting for transfers between devices  164 us
    all_gather x2, waiting for transfers between devices, gather_rows(): lax.all_gather(lines, 'fsdp', axis=0, tiled=False, axis_index_groups=even)  102 us
    reduce_scatter x4, waiting for transfers between devices, scatter_rows(): return lax.psum_scatter(two, 'rep', scatter_dimension=0, tiled=False)  102 us
    all_gather x2, waiting for transfers between devices, gather_rows(): lines = lax.all_gather(packed, 'rep', axis=0, tiled=False)  91.5 us
    all_gather x1, blocking collectives, body(): small_all = lax.all_gather(small, ('fsdp', 'rep'), axis=0, tiled=False)  69.6 us
    unnamed x214, local copies, waits for them, and re-layouts  44.2 us
    dot_general x16, matrix products, dot_tn(): lax.dot_general(left, right, (((0,), (0,)), ((), ())), preferred_element_...  41.3 us
  transfers between devices with their start and end apart: 19, of which 11 were waited for; matrix products, arithmetic and copies ran while one was open for 21% of the time, Pallas kernels for 21%

profile of v1, /device:TPU:0, one launch (start us, length us, event | category | flops | bytes accessed | tf_op | source)
XLA Modules:
  0.0 1039.4 jit_solution(1613313159328930430)
XLA Ops:
  14.3 40.0 %all-gather.10.cloned.1.call-done = bf16[1152,768]{1,0:T(8,128)(2,1)} async-done(((bf16[288,768]{1,0:T(8,128)(2,1)}), bf16[1152,768]{1,0:T(8,128)(2,1)}) %all-gather.10.cloned.1.call-update) | async-done | bytes 1769488 | tf_op jit(solution)/shard_map/all_gather | solution.py:542
  54.4 51.5 %all-gather.14.cloned.1.call-done = bf16[1536,768]{1,0:T(8,128)(2,1)} async-done(((bf16[384,768]{1,0:T(8,128)(2,1)}), bf16[1536,768]{1,0:T(8,128)(2,1)}) %all-gather.14.cloned.1.call-update) | async-done | bytes 2359312 | tf_op jit(solution)/shard_map/all_gather | solution.py:542
  105.9 77.3 %all-gather.12.cloned.1.call-done = bf16[16,288,768]{2,1,0:T(8,128)(2,1)} async-done(((bf16[4,288,768]{2,1,0:T(8,128)(2,1)}), bf16[16,288,768]{2,1,0:T(8,128)(2,1)}) %all-gather.12.cloned.1.call-update) | async-done | bytes 7077904 | tf_op jit(solution)/shard_map/all_gather | solution.py:543
  183.6 69.6 %all-gather.4 = bf16[32,1,696]{2,1,0:T(2,128)(2,1)S(1)} all-gather(bf16[1,1,696]{2,1,0:T(2,128)(2,1)S(1)} %bitcast.305), channel_id=1, replica_groups=mesh['fsdp'=8,'rep'=4] {'fsdp','rep'}, dimensions={0}, use_global_device_ids=true | all-gather | bytes 45936 | tf_op jit(solution)/shard_map/all_gather | solution.py:629
  256.8 24.9 %all-gather.16.cloned.1.call-done = bf16[16,384,768]{2,1,0:T(8,128)(2,1)} async-done(((bf16[4,384,768]{2,1,0:T(8,128)(2,1)}), bf16[16,384,768]{2,1,0:T(8,128)(2,1)}) %all-gather.16.cloned.1.call-update) | async-done | bytes 9437200 | tf_op jit(solution)/shard_map/all_gather | solution.py:543
  281.7 5.8 select_bitcast_fusion.3
  299.0 7.1 shard_map.288
  308.9 29.2 %shard_map.289 = (bf16[1024,768]{1,0:T(8,128)(2,1)S(1)}, f32[16,1024]{1,0:T(8,128)S(1)}) custom-call(bf16[1024,768]{1,0:T(8,128)(2,1)S(1)} %copy-done.64, bf16[1024,768]{1,0:T(8,128)(2,1)S(1)} %copy-done.65, bf16[1024,768]{1,0:T(8,128)(2,1)} %get-tuple-element.84.refs_2_), custom_call_target="tpu_custom_call" | custom-call | flops 12884901888 | bytes 6356992 | tf_op jit(solution)/shard_map/pallas_call | solution.py:49
  339.2 34.6 %shard_map.290 = (f32[1024,768]{1,0:T(8,128)}, bf16[1024,768]{1,0:T(8,128)(2,1)}, bf16[1024,3072]{1,0:T(8,128)(2,1)}, bf16[1024,3072]{1,0:T(8,128)(2,1)}, bf16[1...) custom-call(bf16[1024,768]{1,0:T(8,128)(2,1)} %bitcast.228, ...), custom_call_target="tpu_custom_call" | custom-call | flops 21743271936 | bytes 42147840 | tf_op jit(solution)/shard_map/pallas_call | solution.py:49
  373.9 9.3 convolution_convert_fusion.3
  383.2 7.0 convolution_convert_fusion.2
  390.2 41.1 %shard_map.291 = (bf16[1024,768]{1,0:T(8,128)(2,1)S(1)}, bf16[1024,768]{1,0:T(8,128)(2,1)S(1)}, bf16[1024,768]{1,0:T(8,128)(2,1)S(1)}) custom-call(bf16[1024,768]{1,0:T(8,128)(2,1)} %get-tuple-element.82.refs_0_, bf16[1024,768]{1,0:T(8,128)(2,1)} %get-tuple-element.83.refs_1_, bf16[1024,768]{1,0:T(8,128)(2,1)} %get-tuple-element.84.refs_2_, ...), custom_call_target="tpu_custom_call" | custom-call | flops 32212254720 | bytes 12648448 | tf_op jit(solution)/shard_map/pallas_call | solution.py:49
  441.9 9.8 reshape.377
  451.7 3.2 copy.136
  455.0 5.9 fusion.6
  460.9 4.1 bitcast_add_fusion.1
  485.2 8.7 shard_map.292
  494.5 7.3 fusion.9
  501.9 7.5 select_bitcast_fusion.1
  509.5 8.3 pad_maximum_fusion
  517.8 8.4 fusion.12
  526.2 8.6 slice.251
  534.9 4.7 copy.134
  539.5 3.5 copy.148
  547.3 4.9 shard_map.293
  553.1 10.4 shard_map.294
  567.3 4.6 shard_map.296
  572.0 14.0 %shard_map.297 = (bf16[448,768]{1,0:T(8,128)(2,1)S(1)}, f32[16,448]{1,0:T(8,128)S(1)}) custom-call(bf16[448,768]{1,0:T(8,128)(2,1)S(1)} %get-tuple-element.105.refs_0_, bf16[1024,768]{1,0:T(8,128)(2,1)S(1)} %get-tuple-element.106.refs_1_, bf16[1024,768]{1,0:T(8,128)(2,1)S(1)} %get-tuple-element.107.refs_2_), custom_call_target="tpu_custom_call" | custom-call | flops 5637144576 | bytes 4550656 | tf_op jit(solution)/shard_map/pallas_call | solution.py:49
  587.5 19.8 %shard_map.298 = (f32[448,768]{1,0:T(8,128)}, bf16[448,768]{1,0:T(8,128)(2,1)}, bf16[448,3072]{1,0:T(8,128)(2,1)}, bf16[448,3072]{1,0:T(8,128)(2,1)}, bf16[448,7...) custom-call(f32[448,768]{1,0:T(8,128)} %get-tuple-element.104.x_ref., ...), custom_call_target="tpu_custom_call" | custom-call | flops 9512681472 | bytes 25141248 | tf_op jit(solution)/shard_map/pallas_call | solution.py:49
  607.4 7.0 convolution_convert_fusion.1
  614.4 4.3 convolution_convert_fusion
  618.7 9.8 reshape.387
  628.5 3.4 copy.141
  635.1 19.4 %shard_map.299 = (bf16[448,768]{1,0:T(8,128)(2,1)S(1)}, bf16[1024,768]{1,0:T(8,128)(2,1)S(1)}, bf16[1024,768]{1,0:T(8,128)(2,1)S(1)}) custom-call(bf16[448,768]{1,0:T(8,128)(2,1)S(1)} %copy-done.39, bf16[1024,768]{1,0:T(8,128)(2,1)} %copy-done.62, bf16[1024,768]{1,0:T(8,128)(2,1)} %copy-done.63, bf16[448,768]{1,0:T(8,128)(2,1)S(1)} %copy-done.44, ...), custom_call_target="tpu_custom_call" | custom-call | flops 14092861440 | bytes 9072640 | tf_op jit(solution)/shard_map/pallas_call | solution.py:49
  656.8 4.3 shard_map.300
  664.7 6.7 fusion.4
  677.0 9.9 shard_map.301
  697.7 3.3 copy-done.75
  700.9 7.9 collective-permute-done.4
  708.8 5.1 bitcast_add_fusion
  741.8 5.7 shard_map.302
  747.6 4.2 shard_map.303
  755.1 33.7 %reduce-scatter.29.cloned.1.call-done = bf16[1,4,192,768]{3,2,1,0:T(8,128)(2,1)} async-done(((bf16[4,4,192,768]{3,2,1,0:T(8,128)(2,1)}), bf16[1,4,192,768]{3,2,1,0:T(8,128)(2,1)}) %reduce-scatter.29.cloned.1.call-update) | async-done | bytes 1179664
  788.9 128.6 %all-reduce.12.cloned.1.call-done = f32[32,8,128]{2,1,0:T(8,128)} async-done(((f32[32,8,128]{2,1,0:T(8,128)}), f32[32,8,128]{2,1,0:T(8,128)}) %all-reduce.12.cloned.1.call-update) | async-done | bytes 131088
  920.7 19.9 %reduce-scatter.17.cloned.1.call-done = bf16[1,96,768]{2,1,0:T(8,128)(2,1)} async-done(((bf16[4,96,768]{2,1,0:T(8,128)(2,1)}), bf16[1,96,768]{2,1,0:T(8,128)(2,1)}) %reduce-scatter.17.cloned.1.call-update) | async-done | bytes 147472 | tf_op jit(solution)/shard_map/reduce_scatter | solution.py:559
  942.3 28.2 %reduce-scatter.19.cloned.1.call-done = bf16[1,192,768]{2,1,0:T(8,128)(2,1)} async-done(((bf16[4,192,768]{2,1,0:T(8,128)(2,1)}), bf16[1,192,768]{2,1,0:T(8,128)(2,1)}) %reduce-scatter.19.cloned.1.call-update) | async-done | bytes 294928 | tf_op jit(solution)/shard_map/reduce_scatter | solution.py:559
  973.9 26.7 %reduce-scatter.23.cloned.1.call-done = bf16[1,192,768]{2,1,0:T(8,128)(2,1)} async-done(((bf16[4,192,768]{2,1,0:T(8,128)(2,1)}), bf16[1,192,768]{2,1,0:T(8,128)(2,1)}) %reduce-scatter.23.cloned.1.call-update) | async-done | bytes 294928 | tf_op jit(solution)/shard_map/reduce_scatter | solution.py:559
  1004.0 26.8 %reduce-scatter.21.cloned.1.call-done = bf16[1,192,768]{2,1,0:T(8,128)(2,1)} async-done(((bf16[4,192,768]{2,1,0:T(8,128)(2,1)}), bf16[1,192,768]{2,1,0:T(8,128)(2,1)}) %reduce-scatter.21.cloned.1.call-update) | async-done | bytes 294928 | tf_op jit(solution)/shard_map/reduce_scatter | solution.py:559
  (366 shorter events, 137.8 us)
Async XLA Ops:
  7.2 47.1 %all-gather.10.cloned.1.call-start = ((), (), s32[]{:S(2)}) async-start(), calls=%async_computation.12 | async-start | bytes 2211840 | tf_op jit(solution)/shard_map/all_gather | solution.py:542
  10.3 173.0 %copy-start.88 = (f32[8,24]{1,0:T(8,128)S(1)}, f32[8,24]{1,0:T(8,128)}, u32[]{:S(2)}) copy-start(f32[8,24]{1,0:T(8,128)} %param.24) | copy-start | bytes 2308
  10.3 173.1 %copy-start.87 = (f32[12,24]{1,0:T(8,128)S(1)}, f32[12,24]{1,0:T(8,128)}, u32[]{:S(2)}) copy-start(f32[12,24]{1,0:T(8,128)} %param.29) | copy-start | bytes 3460
  10.3 173.2 %copy-start.94 = (f32[24]{0:T(128)S(1)}, f32[24]{0:T(128)}, u32[]{:S(2)}) copy-start(f32[24]{0:T(128)} %param.31) | copy-start | bytes 292
  10.3 173.2 %copy-start.91 = (f32[96]{0:T(128)S(1)}, f32[96]{0:T(128)}, u32[]{:S(2)}) copy-start(f32[96]{0:T(128)} %param.30) | copy-start | bytes 1156
  10.3 173.2 %copy-start.92 = (f32[96]{0:T(128)S(1)}, f32[96]{0:T(128)}, u32[]{:S(2)}) copy-start(f32[96]{0:T(128)} %param.25) | copy-start | bytes 1156
  11.1 94.7 %all-gather.14.cloned.1.call-start = ((), (), s32[]{:S(2)}) async-start(), calls=%async_computation.14 | async-start | bytes 2949120 | tf_op jit(solution)/shard_map/all_gather | solution.py:542
  12.3 243.8 %copy-start.89 = (pred[8]{0:T(512)(128)(4,1)S(1)}, pred[8]{0:T(512)(128)(4,1)}, u32[]{:S(2)}) copy-start(pred[8]{0:T(512)(128)(4,1)} %constant.59.clone.1) | copy-start | bytes 28
  12.3 243.8 %copy-start.90 = (pred[8]{0:T(512)(128)(4,1)S(1)}, pred[8]{0:T(512)(128)(4,1)}, u32[]{:S(2)}) copy-start(pred[8]{0:T(512)(128)(4,1)} %constant.52.clone.1) | copy-start | bytes 28
  14.2 169.0 %all-gather.12.cloned.1.call-start = ((), (), s32[]{:S(2)}) async-start(), calls=%async_computation.13 | async-start | bytes 8847360 | tf_op jit(solution)/shard_map/all_gather | solution.py:543
  54.3 227.4 %all-gather.16.cloned.1.call-start = ((), (), s32[]{:S(2)}) async-start(), calls=%async_computation.15 | async-start | bytes 11796480 | tf_op jit(solution)/shard_map/all_gather | solution.py:543
  105.9 647.4 %reduce-scatter.25.cloned.1.call-start = ((), (), s32[]{:S(2)}) async-start(), calls=%async_computation.17 | async-start | bytes 2949120
  183.2 98.5 %collective-permute-start = (bf16[4,4,288,768]{3,2,1,0:T(8,128)(2,1)}, bf16[4,4,288,768]{3,2,1,0:T(8,128)(2,1)}, u32[]{:S(2)}, u32[]{:S(2)}) collective-permute-start(bf16[4,4,288,768]{3,2,1,0:T(8,128)(2,1)} %bitcast.251), channel_id=1, source_target_pairs={{0,4},{4,0},{8,12},{12,8},{16,20},{20,16},{24,28},{28,24},{1,5},{5... | collective-permute-start | bytes 21233672 | tf_op jit(solution)/shard_map/ppermute | solution.py:544
  255.0 32.5 %copy-start.76 = (f32[32,288]{0,1:T(8,128)}, f32[32,288]{0,1:T(8,128)S(1)}, u32[]{:S(2)}) copy-start(f32[32,288]{0,1:T(8,128)S(1)} %copy.126) | copy-start | bytes 110596
  281.7 220.2 %collective-permute-start.1 = (bf16[4,4,384,768]{3,2,1,0:T(8,128)(2,1)}, bf16[4,4,384,768]{3,2,1,0:T(8,128)(2,1)}, u32[]{:S(2)}, u32[]{:S(2)}) collective-permute-start(bf16[4,4,384,768]{3,2,1,0:T(8,128)(2,1)} %bitcast.249), channel_id=1, source_target_pairs={{0,4},{4,0},{8,12},{12,8},{16,20},{20,16},{24,28},{28,24},{1,5},{5... | collective-permute-start | bytes 28311560 | tf_op jit(solution)/shard_map/ppermute | solution.py:544
  373.9 9.3 copy-start.98
  373.9 9.3 copy-start.100
  390.2 41.2 %copy-start.61 = (bf16[1024,768]{1,0:T(8,128)(2,1)S(1)}, bf16[1024,768]{1,0:T(8,128)(2,1)}, u32[]{:S(2)}) copy-start(bf16[1024,768]{1,0:T(8,128)(2,1)} %copy-done.60) | copy-start | bytes 4718596
  390.2 41.2 %copy-start.96 = (bf16[1024,768]{1,0:T(8,128)(2,1)S(1)}, bf16[1024,768]{1,0:T(8,128)(2,1)}, u32[]{:S(2)}) copy-start(bf16[1024,768]{1,0:T(8,128)(2,1)} %get-tuple-element.131) | copy-start | bytes 4718596
  441.4 19.4 %collective-permute-start.2 = (bf16[4,4,96,768]{3,2,1,0:T(8,128)(2,1)}, bf16[4,4,96,768]{3,2,1,0:T(8,128)(2,1)}, u32[]{:S(2)}, u32[]{:S(2)}) collective-permute-start(bf16[4,4,96,768]{3,2,1,0:T(8,128)(2,1)} %dynamic-slice_bitcast_fusion.1), channel_id=1, source_target_pairs={{0,4},{4,0},{8,12},{12,8},{16,20},{20,16},{24,28},{28,24},{1,5},{5... | collective-permute-start | bytes 7077896 | tf_op jit(solution)/shard_map/ppermute | solution.py:557
  460.8 33.7 %collective-permute-start.3 = (bf16[4,4,192,768]{3,2,1,0:T(8,128)(2,1)}, bf16[4,4,192,768]{3,2,1,0:T(8,128)(2,1)}, u32[]{:S(2)}, u32[]{:S(2)}) collective-permute-start(bf16[4,4,192,768]{3,2,1,0:T(8,128)(2,1)} %fusion.6), channel_id=1, source_target_pairs={{0,4},{4,0},{8,12},{12,8},{16,20},{20,16},{24,28},{28,24},{1,5},{5... | collective-permute-start | bytes 14155784 | tf_op jit(solution)/shard_map/ppermute | solution.py:557
  460.9 20.0 %copy-start.28 = (s32[1,448]{1,0:T(1,128)S(1)}, s32[1,448]{1,0:T(1,128)}, u32[]{:S(2)}) copy-start(s32[1,448]{1,0:T(1,128)} %refs_7_.1) | copy-start | bytes 5380
  465.0 288.8 %reduce-scatter.27.cloned.1.call-start = ((), (), s32[]{:S(2)}) async-start(), calls=%async_computation.18 | async-start | bytes 5898240
  501.9 252.7 %reduce-scatter.31.cloned.1.call-start = ((), (), s32[]{:S(2)}) async-start(), calls=%async_computation.20 | async-start | bytes 5898240
  547.3 16.2 %copy-start = (bf16[1,32,24,768]{3,2,0,1:T(8,128)(2,1)}, bf16[1,32,24,768]{3,2,0,1:T(8,128)(2,1)S(1)}, u32[]{:S(2)}) copy-start(bf16[1,32,24,768]{3,2,0,1:T(8,128)(2,1)S(1)} %get-tuple-element.161) | copy-start | bytes 3538948
  547.3 20.0 %copy-start.3 = (bf16[1,32,24,768]{3,2,0,1:T(8,128)(2,1)}, bf16[1,32,24,768]{3,2,0,1:T(8,128)(2,1)S(1)}, u32[]{:S(2)}) copy-start(bf16[1,32,24,768]{3,2,0,1:T(8,128)(2,1)S(1)} %get-tuple-element.158) | copy-start | bytes 3538948
  547.3 20.0 %copy-start.5 = (bf16[1,32,24,768]{3,2,0,1:T(8,128)(2,1)}, bf16[1,32,24,768]{3,2,0,1:T(8,128)(2,1)S(1)}, u32[]{:S(2)}) copy-start(bf16[1,32,24,768]{3,2,0,1:T(8,128)(2,1)S(1)} %get-tuple-element.159) | copy-start | bytes 3538948
  553.1 10.4 %copy-start.50 = (bf16[448,768]{1,0:T(8,128)(2,1)}, bf16[448,768]{1,0:T(8,128)(2,1)S(1)}, u32[]{:S(2)}) copy-start(bf16[448,768]{1,0:T(8,128)(2,1)S(1)} %get-tuple-element.101.refs_1_) | copy-start | bytes 2064388
  553.1 10.4 %copy-start.52 = (bf16[448,768]{1,0:T(8,128)(2,1)}, bf16[448,768]{1,0:T(8,128)(2,1)S(1)}, u32[]{:S(2)}) copy-start(bf16[448,768]{1,0:T(8,128)(2,1)S(1)} %get-tuple-element.102.refs_2_) | copy-start | bytes 2064388
  553.1 13.3 %copy-start.48 = (bf16[448,768]{1,0:T(8,128)(2,1)}, bf16[448,768]{1,0:T(8,128)(2,1)S(1)}, u32[]{:S(2)}) copy-start(bf16[448,768]{1,0:T(8,128)(2,1)S(1)} %get-tuple-element.100.refs_0_) | copy-start | bytes 2064388
  553.1 10.4 %copy-start.20 = (f32[8,768]{1,0:T(8,128)S(1)}, f32[8,768]{1,0:T(8,128)}, u32[]{:S(2)}) copy-start(f32[8,768]{1,0:T(8,128)} %pad.36.vec_ref) | copy-start | bytes 73732
  553.1 14.2 %copy-start.25 = (f32[8,768]{1,0:T(8,128)S(1)}, f32[8,768]{1,0:T(8,128)}, u32[]{:S(2)}) copy-start(f32[8,768]{1,0:T(8,128)} %pad.37.vec_ref) | copy-start | bytes 73732
  567.3 18.7 %copy-start.38 = (bf16[448,768]{1,0:T(8,128)(2,1)}, bf16[448,768]{1,0:T(8,128)(2,1)S(1)}, u32[]{:S(2)}) copy-start(bf16[448,768]{1,0:T(8,128)(2,1)S(1)} %get-tuple-element.105.refs_0_) | copy-start | bytes 2064388
  572.0 14.0 %copy-start.62 = (bf16[1024,768]{1,0:T(8,128)(2,1)}, bf16[1024,768]{1,0:T(8,128)(2,1)S(1)}, u32[]{:S(2)}) copy-start(bf16[1024,768]{1,0:T(8,128)(2,1)S(1)} %get-tuple-element.106.refs_1_) | copy-start | bytes 4718596
  572.0 14.0 %copy-start.63 = (bf16[1024,768]{1,0:T(8,128)(2,1)}, bf16[1024,768]{1,0:T(8,128)(2,1)S(1)}, u32[]{:S(2)}) copy-start(bf16[1024,768]{1,0:T(8,128)(2,1)S(1)} %get-tuple-element.107.refs_2_) | copy-start | bytes 4718596
  634.7 29.9 %collective-permute-start.5 = (bf16[4,4,192,768]{3,2,1,0:T(8,128)(2,1)}, bf16[4,4,192,768]{3,2,1,0:T(8,128)(2,1)}, u32[]{:S(2)}, u32[]{:S(2)}) collective-permute-start(bf16[4,4,192,768]{3,2,1,0:T(8,128)(2,1)} %fusion.1), channel_id=1, source_target_pairs={{0,4},{4,0},{8,12},{12,8},{16,20},{20,16},{24,28},{28,24},{1,5},{5... | collective-permute-start | bytes 14155784 | tf_op jit(solution)/shard_map/ppermute | solution.py:557
  635.1 21.8 %copy-start.1 = (bf16[1,32,24,768]{3,2,0,1:T(8,128)(2,1)S(1)}, bf16[1,32,24,768]{3,2,0,1:T(8,128)(2,1)}, u32[]{:S(2)}) copy-start(bf16[1,32,24,768]{3,2,0,1:T(8,128)(2,1)} %copy-done) | copy-start | bytes 3538948
  635.1 21.8 %copy-start.21 = (f32[8,768]{1,0:T(8,128)S(1)}, f32[8,768]{1,0:T(8,128)}, u32[]{:S(2)}) copy-start(f32[8,768]{1,0:T(8,128)} %pad.36.vec_ref) | copy-start | bytes 73732
  671.4 117.4 %reduce-scatter.29.cloned.1.call-start = ((), (), s32[]{:S(2)}) async-start(), calls=%async_computation.19 | async-start | bytes 5898240
  677.0 9.9 copy-start.47
  700.9 7.9 collective-permute-start.4
  714.0 33.6 %copy-start.4 = (bf16[1,32,24,768]{3,2,0,1:T(8,128)(2,1)S(1)}, bf16[1,32,24,768]{3,2,0,1:T(8,128)(2,1)}, u32[]{:S(2)}) copy-start(bf16[1,32,24,768]{3,2,0,1:T(8,128)(2,1)} %copy-done.3) | copy-start | bytes 3538948
  714.0 203.5 %all-reduce.12.cloned.1.call-start = ((), (), s32[]{:S(2)}) async-start(), calls=%async_computation.16 | async-start | bytes 262144
  736.4 11.2 %copy-start.6 = (bf16[1,32,24,768]{3,2,0,1:T(8,128)(2,1)S(1)}, bf16[1,32,24,768]{3,2,0,1:T(8,128)(2,1)}, u32[]{:S(2)}) copy-start(bf16[1,32,24,768]{3,2,0,1:T(8,128)(2,1)} %copy-done.5) | copy-start | bytes 3538948
  753.2 187.5 %reduce-scatter.17.cloned.1.call-start = ((), (), s32[]{:S(2)}) async-start(), calls=%async_computation.8 | async-start | bytes 737280 | tf_op jit(solution)/shard_map/reduce_scatter | solution.py:559
  753.8 216.7 %reduce-scatter.19.cloned.1.call-start = ((), (), s32[]{:S(2)}) async-start(), calls=%async_computation.9 | async-start | bytes 1474560 | tf_op jit(solution)/shard_map/reduce_scatter | solution.py:559
  754.5 246.1 %reduce-scatter.23.cloned.1.call-start = ((), (), s32[]{:S(2)}) async-start(), calls=%async_computation.11 | async-start | bytes 1474560 | tf_op jit(solution)/shard_map/reduce_scatter | solution.py:559
  755.1 275.7 %reduce-scatter.21.cloned.1.call-start = ((), (), s32[]{:S(2)}) async-start(), calls=%async_computation.10 | async-start | bytes 1474560 | tf_op jit(solution)/shard_map/reduce_scatter | solution.py:559
  (72 other events, 185.3 us)
Sparse Core Ops, SparseCore 0:
  11.3 43.0 all-gather.9
  56.4 49.3 all-gather.13
  107.7 75.4 all-gather.11
  184.9 96.7 all-gather.15
  465.1 37.5 reduce-scatter.24
  505.5 57.0 reduce-scatter.26
  671.5 57.1 reduce-scatter.30
  731.7 57.0 reduce-scatter.28
  795.0 122.4 all-reduce.11
  919.6 21.0 reduce-scatter.16
  943.0 27.4 reduce-scatter.18
  972.7 27.8 reduce-scatter.22
  1002.9 27.8 reduce-scatter.20
